TPU v7x, 32 devices: a whole 2x2x4 slice. The times are simulated.
32 devices in a mesh: layer: 2 (over core), prow: 4 (over z), pcol: 4 (over y, x).
Axes of the slice: x: 2, y: 2, z: 4, core: 2. Of those that a mesh axis runs over, the one named last changes fastest.
Arguments:
- factor: bfloat16 [2, 4, 4, 4, 4, 256, 256], P('layer', 'prow', None, None, 'pcol'), may hold values from -0.1875 to 0.1875
- factor_scale: float32 [2, 4, 4, 4, 4], P('layer', 'prow', None, None, 'pcol'), may hold values from 0.25 to 4
- sub_pattern: int32 [2, 4, 4, 4, 4], P('layer', 'prow', None, None, 'pcol'), may hold values from 0 to 1, as said below
- coupling: bfloat16 [2, 4, 4, 4, 4, 256, 256], P('layer', 'prow', None, None, 'pcol'), may hold values from -0.1875 to 0.1875
- coupling_scale: float32 [2, 4, 4, 4, 4], P('layer', 'prow', None, None, 'pcol'), may hold values from 0.25 to 4
- top_pattern: int32 [2, 4, 4, 4, 4], P('layer', 'prow', None, None, 'pcol'), may hold values 0 or 1
- diag_inverse: float32 [2, 4, 4, 256, 256], P('layer', 'prow', 'pcol'), may hold values from -1 to 2
- top_inverse: float32 [4, 4, 256, 256], P('prow', 'pcol'), may hold values from -1 to 2
- rhs_sub: float32 [2, 4, 4, 256, 256], P('layer', 'prow', 'pcol'), may hold values from -6 to 6
- rhs_top: float32 [4, 4, 256, 256], P('prow', 'pcol'), may hold values from -6 to 6
Outputs:
- sol_sub: float32 [2, 4, 4, 256, 256], P('layer', 'prow', 'pcol')
- sol_top: float32 [4, 4, 256, 256], P('prow', 'pcol')
Inputs may be any that keep to these rules, and one draw needn't show every extreme that they name: The supernodes of each layer fall into 3 levels; sub_pattern is 1 only where the column supernode's level is below the row supernode's level.
All inputs are finite; a program needn't handle non-finite values. No bound on the sum of `top_pattern` on one device may be relied on, other than what follows from the above.
Results may differ from a plain program's by a relative error of at most 0.02.
Values may be sent and summed in bfloat16 or wider, within the bound.
No kernel may reach another device: no remote copies, remote signals or barrier semaphores. Data moves between devices by JAX's collectives and lax.ppermute only.
A program may use at most 64 MiB of HBM per device.

v0:
```python
import jax
import jax.numpy as jnp
from jax import lax
from jax.sharding import PartitionSpec as P

LEVELS = 3


HIGH_PREC = lax.Precision.HIGHEST


def apply_left(matrix, values):
    return jnp.dot(matrix, values, precision=HIGH_PREC, preferred_element_type=jnp.float32)


def apply_trans(matrix, values):
    return jnp.dot(matrix.T, values, precision=HIGH_PREC, preferred_element_type=jnp.float32)


def forward_partial(values, matrices, scaling):
    shared = values.astype(jnp.bfloat16)[None]
    products = jnp.einsum(
        "bawk,akr->bawr",
        matrices,
        lax.all_gather(shared, "prow", axis=0, tiled=True),
        preferred_element_type=jnp.float32,
    )
    return jnp.sum(products * scaling[:, :, None, None], axis=1)


def column_total(values, matrices, scaling):
    shared = values.astype(jnp.bfloat16)[None]
    products = jnp.einsum(
        "bakw,bkr->bawr",
        matrices,
        lax.all_gather(shared, "pcol", axis=0, tiled=True),
        preferred_element_type=jnp.float32,
    )
    partial_value = jnp.sum(products * scaling[:, :, None, None], axis=0)
    return lax.psum_scatter(
        partial_value.astype(jnp.bfloat16), "prow", scatter_dimension=0, tiled=True
    ).astype(jnp.float32)[0]


def shards(
    factor,
    factor_scale,
    sub_pattern,
    coupling,
    coupling_scale,
    top_pattern,
    diag_inverse,
    top_inverse,
    rhs_sub,
    rhs_top,
):
    super_width = factor.shape[5]
    row_count = factor.shape[2]
    col_count = factor.shape[3]
    factor_blocks = factor.reshape(row_count, col_count, super_width, super_width)
    factor_weights = (factor_scale * sub_pattern.astype(jnp.float32)).reshape(row_count, col_count)
    link_blocks = coupling.reshape(row_count, col_count, super_width, super_width)
    link_weights = (coupling_scale * top_pattern.astype(jnp.float32)).reshape(row_count, col_count)
    inverse = diag_inverse.reshape(super_width, super_width)
    top_matrix = top_inverse.reshape(super_width, super_width)
    own_rhs = rhs_sub.reshape(super_width, rhs_sub.shape[-1])
    top_rhs = rhs_top.reshape(super_width, rhs_top.shape[-1])
    solved = apply_left(inverse, own_rhs)
    for sweep_index in range(LEVELS - 1):
        partial_value = forward_partial(solved, factor_blocks, factor_weights)
        lower_sum = lax.psum_scatter(
            partial_value.astype(jnp.bfloat16), "pcol", scatter_dimension=0, tiled=True
        ).astype(jnp.float32)[0]
        solved = apply_left(inverse, own_rhs - lower_sum)
    top_partial = forward_partial(solved, link_blocks, link_weights)
    top_part = lax.psum_scatter(
        top_partial.astype(jnp.bfloat16), "pcol", scatter_dimension=0, tiled=True
    ).astype(jnp.float32)[0]
    merged = lax.psum(top_part.astype(jnp.bfloat16), "layer").astype(jnp.float32)
    top_fwd = apply_left(top_matrix, top_rhs - merged)
    top_answer = apply_trans(top_matrix, top_fwd)
    coupled = column_total(top_answer, link_blocks, link_weights)
    answer = apply_trans(inverse, solved - coupled)
    for sweep_index in range(LEVELS - 1):
        upper_sum = column_total(answer, factor_blocks, factor_weights)
        answer = apply_trans(inverse, solved - coupled - upper_sum)
    return (answer.reshape(rhs_sub.shape), top_answer.reshape(rhs_top.shape))


def solution(mesh):
    return jax.shard_map(
        shards,
        mesh=mesh,
        in_specs=(
            P("layer", "prow", None, None, "pcol", None, None),
            P("layer", "prow", None, None, "pcol"),
            P("layer", "prow", None, None, "pcol"),
            P("layer", "prow", None, None, "pcol", None, None),
            P("layer", "prow", None, None, "pcol"),
            P("layer", "prow", None, None, "pcol"),
            P("layer", "prow", "pcol", None, None),
            P("prow", "pcol", None, None),
            P("layer", "prow", "pcol", None, None),
            P("prow", "pcol", None, None),
        ),
        out_specs=(P("layer", "prow", "pcol", None, None), P("prow", "pcol", None, None)),
        check_vma=False,
    )
```

profile of v0, /device:TPU:0, one launch (start us, length us, event | category | flops | bytes accessed | tf_op | source)
XLA Modules:
  0.0 298.1 jit_solution(12780264937894898415)
XLA Ops:
  7.2 0.0 copy-start
  7.2 0.0 reduce-scatter.19.cloned.1.call-start
  7.2 0.8 convert_multiply_fusion.1
  8.1 0.1 copy.27
  8.2 1.4 convolution_convert_fusion.3
  9.6 17.4 %all-gather = bf16[1024,256]{1,0:T(8,128)(2,1)S(1)} all-gather(bf16[256,256]{1,0:T(8,128)(2,1)S(1)} %convolution_convert_fusion.3), channel_id=2, replica_groups=mesh['layer'=2,'prow'=4,'pcol'=4] {'prow'}, dimensions={0}, use_global_device_ids=true | all-gather | bytes 655360 | tf_op jit(solution)/shard_map/all_gather | solution.py:25
  27.0 0.0 copy-done
  27.0 0.0 copy-start.1
  27.0 0.9 fusion.2
  27.9 1.0 copy.28
  28.9 0.0 reduce-scatter.19.cloned.1.call-update
  28.9 0.0 reduce-scatter.21.cloned.1.call-start
  28.9 27.0 %reduce-scatter.19.cloned.1.call-done = bf16[1,256,256]{2,1,0:T(8,128)(2,1)} async-done(((bf16[4,256,256]{2,1,0:T(8,128)(2,1)}), bf16[1,256,256]{2,1,0:T(8,128)(2,1)}) %reduce-scatter.19.cloned.1.call-update) | async-done | bytes 131088
  55.9 0.0 copy-done.1
  55.9 0.0 copy-done.2
  55.9 1.5 fusion.6
  57.4 15.4 %all-gather.1 = bf16[1024,256]{0,1:T(8,128)(2,1)S(1)} all-gather(bf16[256,256]{0,1:T(8,128)(2,1)S(1)} %fusion.6), channel_id=3, replica_groups=mesh['layer'=2,'prow'=4,'pcol'=4] {'prow'}, dimensions={0}, use_global_device_ids=true | all-gather | bytes 655360 | tf_op jit(solution)/shard_map/all_gather | solution.py:25
  72.8 1.2 reshape.51
  74.0 1.9 fusion.1
  75.9 1.0 copy.31
  76.8 0.0 reduce-scatter.21.cloned.1.call-update
  76.9 0.0 reduce-scatter.23.cloned.1.call-start
  76.9 0.0 copy-done.6
  76.9 0.0 copy-done.7
  77.0 0.1 copy.34
  77.0 25.9 %reduce-scatter.21.cloned.1.call-done = bf16[1,256,256]{2,1,0:T(8,128)(2,1)} async-done(((bf16[4,256,256]{2,1,0:T(8,128)(2,1)}), bf16[1,256,256]{2,1,0:T(8,128)(2,1)}) %reduce-scatter.21.cloned.1.call-update) | async-done | bytes 131088
  102.9 1.5 fusion.37
  104.4 15.4 %all-gather.2 = bf16[1024,256]{0,1:T(8,128)(2,1)S(1)} all-gather(bf16[256,256]{0,1:T(8,128)(2,1)S(1)} %get-tuple-element.6), channel_id=4, replica_groups=mesh['layer'=2,'prow'=4,'pcol'=4] {'prow'}, dimensions={0}, use_global_device_ids=true | all-gather | bytes 655360 | tf_op jit(solution)/shard_map/all_gather | solution.py:25
  119.8 1.2 reshape.52
  121.0 3.5 %fusion = bf16[4,256,256]{1,2,0:T(8,128)(2,1)} fusion(f32[4,4]{0,1:T(4,128)S(1)} %copy.34, bf16[4,256,256,1]{1,0,2,3:T(4,128)(2,1)} %bitcast.158, bf16[1,1,4,4,1,256,256]{6,5,4,3,2,1,0:T(8,128)(2,1)} %param.13), kind=kOutput, calls=%fused_computation.1 | convolution fusion | flops 538705920 | bytes 3145792 | tf_op jit(solution)/shard_map/bawk,akr->bawr/dot_general | solution.py:22
  124.5 2.1 copy.35
  126.5 0.0 reduce-scatter.23.cloned.1.call-update
  126.5 0.0 all-reduce.5.cloned.1.call-start
  126.6 26.0 %reduce-scatter.23.cloned.1.call-done = bf16[1,256,256]{2,1,0:T(8,128)(2,1)} async-done(((bf16[4,256,256]{2,1,0:T(8,128)(2,1)}), bf16[1,256,256]{2,1,0:T(8,128)(2,1)}) %reduce-scatter.23.cloned.1.call-update) | async-done | bytes 131088
  152.6 0.0 all-reduce.5.cloned.1.call-update
  152.6 0.0 reduce-scatter.13.cloned.1.call-start
  152.7 20.1 %all-reduce.5.cloned.1.call-done = bf16[256,256]{1,0:T(8,128)(2,1)} async-done(((bf16[256,256]{1,0:T(8,128)(2,1)}), bf16[256,256]{1,0:T(8,128)(2,1)}) %all-reduce.5.cloned.1.call-update) | async-done | bytes 131088 | tf_op jit(solution)/shard_map/psum | solution.py:79
  172.7 0.0 copy-done.4
  172.7 0.0 copy-done.5
  172.7 1.5 fusion.20
  174.2 0.4 bitcast_convert_fusion
  174.6 14.6 %all-gather.3 = bf16[1024,256]{0,1:T(8,128)(2,1)S(1)} all-gather(bf16[256,256]{0,1:T(8,128)(2,1)S(1)} %get-tuple-element.8), channel_id=5, replica_groups=mesh['layer'=2,'prow'=4,'pcol'=4] {'pcol'}, dimensions={0}, use_global_device_ids=true | all-gather | bytes 655360 | tf_op jit(solution)/shard_map/all_gather | solution.py:36
  189.2 1.2 reshape.53
  190.4 3.4 %multiply_reduce_fusion.2 = bf16[256,4,256]{2,0,1:T(8,128)(2,1)} fusion(f32[4,4]{1,0:T(4,128)S(1)} %bitcast.167, bf16[4,256,256,1]{1,0,2,3:T(4,128)(2,1)} %bitcast.159, bf16[1,1,4,4,1,256,256]{6,5,4,3,2,1,0:T(8,128)(2,1)} %param.13), kind=kOutput, calls=%fused_computation.8 | convolution fusion | flops 538705920 | bytes 3145792 | tf_op jit(solution)/shard_map/bakw,bkr->bawr/dot_general | solution.py:33
  193.8 0.0 reduce-scatter.13.cloned.1.call-update
  193.8 0.0 reduce-scatter.15.cloned.1.call-start
  193.9 22.0 %reduce-scatter.13.cloned.1.call-done = bf16[1,256,256]{1,2,0:T(8,128)(2,1)} async-done(((bf16[4,256,256]{1,2,0:T(8,128)(2,1)}), bf16[1,256,256]{1,2,0:T(8,128)(2,1)}) %reduce-scatter.13.cloned.1.call-update) | async-done | bytes 131088 | tf_op jit(solution)/shard_map/reduce_scatter | solution.py:40
  215.8 1.3 fusion.7
  217.1 12.0 %all-gather.4 = bf16[1024,256]{0,1:T(8,128)(2,1)S(1)} all-gather(bf16[256,256]{0,1:T(8,128)(2,1)S(1)} %fusion.7), channel_id=6, replica_groups=mesh['layer'=2,'prow'=4,'pcol'=4] {'pcol'}, dimensions={0}, use_global_device_ids=true | all-gather | bytes 655360 | tf_op jit(solution)/shard_map/all_gather | solution.py:36
  229.1 1.2 reshape.54
  230.3 2.7 multiply_reduce_fusion.1
  233.0 0.0 reduce-scatter.15.cloned.1.call-update
  233.0 0.0 reduce-scatter.17.cloned.1.call-start
  233.1 19.4 %reduce-scatter.15.cloned.1.call-done = bf16[1,256,256]{1,2,0:T(8,128)(2,1)} async-done(((bf16[4,256,256]{1,2,0:T(8,128)(2,1)}), bf16[1,256,256]{1,2,0:T(8,128)(2,1)}) %reduce-scatter.15.cloned.1.call-update) | async-done | bytes 131088 | tf_op jit(solution)/shard_map/reduce_scatter | solution.py:40
  252.4 0.0 copy-done.3
  252.4 1.3 fusion.8
  253.7 12.0 %all-gather.5 = bf16[1024,256]{0,1:T(8,128)(2,1)S(1)} all-gather(bf16[256,256]{0,1:T(8,128)(2,1)S(1)} %fusion.8), channel_id=7, replica_groups=mesh['layer'=2,'prow'=4,'pcol'=4] {'pcol'}, dimensions={0}, use_global_device_ids=true | all-gather | bytes 655360 | tf_op jit(solution)/shard_map/all_gather | solution.py:36
  265.8 1.2 reshape.55
  267.0 2.7 multiply_reduce_fusion
  269.6 0.0 reduce-scatter.17.cloned.1.call-update
  269.7 0.8 copy.40
  270.5 18.6 %reduce-scatter.17.cloned.1.call-done = bf16[1,256,256]{1,2,0:T(8,128)(2,1)} async-done(((bf16[4,256,256]{1,2,0:T(8,128)(2,1)}), bf16[1,256,256]{1,2,0:T(8,128)(2,1)}) %reduce-scatter.17.cloned.1.call-update) | async-done | bytes 131088 | tf_op jit(solution)/shard_map/reduce_scatter | solution.py:40
  289.1 1.3 convolution_bitcast_fusion
  290.4 0.8 copy.39
  (7 shorter events, 0.0 us)
Async XLA Ops:
  7.2 19.8 %copy-start = (bf16[1,1,4,4,1,256,256]{6,5,4,3,2,1,0:T(8,128)(2,1)S(1)}, bf16[1,1,4,4,1,256,256]{6,5,4,3,2,1,0:T(8,128)(2,1)}, u32[]{:S(2)}) copy-start(bf16[1,1,4,4,1,256,256]{6,5,4,3,2,1,0:T(8,128)(2,1)} %param.10) | copy-start | bytes 6291460
  7.2 48.7 %reduce-scatter.19.cloned.1.call-start = ((), (), s32[]{:S(2)}) async-start(), calls=%async_computation.10 | async-start | bytes 655360
  27.0 29.0 %copy-start.1 = (f32[1,1,1,256,256]{4,3,2,1,0:T(8,128)S(1)}, f32[1,1,1,256,256]{4,3,2,1,0:T(8,128)}, u32[]{:S(2)}) copy-start(f32[1,1,1,256,256]{4,3,2,1,0:T(8,128)} %param.16) | copy-start | bytes 786436
  27.0 29.0 %copy-start.2 = (f32[1,1,1,256,256]{4,3,2,1,0:T(8,128)S(1)}, f32[1,1,1,256,256]{4,3,2,1,0:T(8,128)}, u32[]{:S(2)}) copy-start(f32[1,1,1,256,256]{4,3,2,1,0:T(8,128)} %param.18) | copy-start | bytes 786436
  28.9 74.0 %reduce-scatter.21.cloned.1.call-start = ((), (), s32[]{:S(2)}) async-start(), calls=%async_computation.11 | async-start | bytes 655360
  74.0 2.9 copy-start.6
  74.0 3.0 copy-start.7
  76.9 75.7 %reduce-scatter.23.cloned.1.call-start = ((), (), s32[]{:S(2)}) async-start(), calls=%async_computation.12 | async-start | bytes 655360
  121.0 51.7 %copy-start.4 = (f32[1,1,256,256]{3,2,1,0:T(8,128)S(1)}, f32[1,1,256,256]{3,2,1,0:T(8,128)}, u32[]{:S(2)}) copy-start(f32[1,1,256,256]{3,2,1,0:T(8,128)} %param.17) | copy-start | bytes 786436
  121.0 51.7 %copy-start.5 = (f32[1,1,256,256]{3,2,1,0:T(8,128)S(1)}, f32[1,1,256,256]{3,2,1,0:T(8,128)}, u32[]{:S(2)}) copy-start(f32[1,1,256,256]{3,2,1,0:T(8,128)} %param.19) | copy-start | bytes 786436
  126.5 46.2 %all-reduce.5.cloned.1.call-start = ((), (), s32[]{:S(2)}) async-start(), calls=%async_computation.6 | async-start | bytes 262144 | tf_op jit(solution)/shard_map/psum | solution.py:79
  152.6 63.2 %reduce-scatter.13.cloned.1.call-start = ((), (), s32[]{:S(2)}) async-start(), calls=%async_computation.7 | async-start | bytes 655360 | tf_op jit(solution)/shard_map/reduce_scatter | solution.py:40
  193.8 58.6 %reduce-scatter.15.cloned.1.call-start = ((), (), s32[]{:S(2)}) async-start(), calls=%async_computation.8 | async-start | bytes 655360 | tf_op jit(solution)/shard_map/reduce_scatter | solution.py:40
  230.3 22.1 %copy-start.3 = (bf16[1,256,256]{1,2,0:T(8,128)(2,1)S(1)}, bf16[1,256,256]{1,2,0:T(8,128)(2,1)}, u32[]{:S(2)}) copy-start(bf16[1,256,256]{1,2,0:T(8,128)(2,1)} %reduce-scatter.13.cloned.1.call-done) | copy-start | bytes 393220
  233.0 56.1 %reduce-scatter.17.cloned.1.call-start = ((), (), s32[]{:S(2)}) async-start(), calls=%async_computation.9 | async-start | bytes 655360 | tf_op jit(solution)/shard_map/reduce_scatter | solution.py:40
Sparse Core Ops, SparseCore 0:
  29.0 26.8 reduce-scatter.18
  77.0 25.8 reduce-scatter.20
  126.7 25.8 reduce-scatter.22
  154.7 17.9 all-reduce.4
  193.9 21.8 reduce-scatter.12
  233.1 19.2 reduce-scatter.14
  269.8 19.2 reduce-scatter.16
where the time goes:
time: 299 us; the launch traced here: 298 us
  waiting for transfers between devices  159 us (53%)
  blocking collectives  86.8 us (29%)
  matrix products  25.1 us (8%)
  between operations  14.2 us (5%)
  local copies, waits for them, and re-layouts  11.8 us (4%)
    unnamed x10, waiting for transfers between devices  78.9 us
    reduce_scatter x3, waiting for transfers between devices, column_total(): lax.psum_scatter(partial_value.astype(jnp.bfloat16), 'prow', scatter_dime...  59.9 us
    all_gather x3, blocking collectives, forward_partial(): lax.all_gather(shared, 'prow', axis=0, tiled=True)  48.2 us
    all_gather x3, blocking collectives, column_total(): lax.all_gather(shared, 'pcol', axis=0, tiled=True)  38.7 us
    psum x1, waiting for transfers between devices, shards(): lax.psum(top_part.astype(jnp.bfloat16), 'layer').astype(jnp.float32)  20.1 us
    dot_general x3, matrix products, column_total(): jnp.einsum('bakw,bkr->bawr', matrices, lax.all_gather(shared, 'pcol', axi...  8.74 us
    dot_general x3, matrix products, forward_partial(): jnp.einsum('bawk,akr->bawr', matrices, lax.all_gather(shared, 'prow', axi...  6.24 us
  transfers between devices with their start and end apart: 7, of which 7 were waited for; matrix products, arithmetic and copies ran while one was open for 0% of the time, Pallas kernels for 0%

commit v1 on v0

v1 whole, which is shorter than its diff:
```python
import functools

import jax
import jax.numpy as jnp
from jax import lax
from jax.experimental import pallas as pl
from jax.experimental.pallas import tpu as pltpu
from jax.sharding import PartitionSpec as P

LEVELS = 3
CHUNKS = 2
HIGH_PREC = lax.Precision.HIGHEST
ROWS_FIRST = ((1,), (0,))
F32 = jnp.float32
BF16 = jnp.bfloat16

SMEM = pl.BlockSpec(memory_space=pltpu.SMEM)
VMEM = pl.BlockSpec(memory_space=pltpu.VMEM)


def partner(index, step, count):
    if count & (count - 1) == 0:
        return index ^ step
    return (index + step) % count


def source(index, step, count):
    if count & (count - 1) == 0:
        return index ^ step
    return (index + count - step) % count


def exchange(values, axis, count):
    received = [None] * count
    received[0] = values[0]
    for step in reversed(range(1, count)):
        pairs = [(index, partner(index, step, count)) for index in range(count)]
        received[step] = lax.ppermute(values[step], axis, pairs)
    return received


def spread(value, axis, count):
    return exchange([value] * count, axis, count)


def call(body, outs, specs, operands, name, flops):
    size = sum(x.size * x.dtype.itemsize for x in operands)
    return pl.pallas_call(
        body,
        out_shape=[jax.ShapeDtypeStruct(shape, dtype) for shape, dtype in outs],
        in_specs=specs,
        out_specs=[VMEM] * len(outs),
        name=name,
        cost_estimate=pl.CostEstimate(flops=flops, bytes_accessed=size, transcendentals=0),
        compiler_params=pltpu.CompilerParams(vmem_limit_bytes=16 * 1024 * 1024),
    )(*operands)


def solve_dot(a, b):
    return jnp.dot(a, b, precision=HIGH_PREC, preferred_element_type=F32)


def total_of(refs):
    total = refs[0][...].astype(F32)
    for ref in refs[1:]:
        total = total + ref[...].astype(F32)
    return total


def forward_products(blocks, weights, fields, rows, cols):
    size, width = fields[0].shape

    def body(weight_ref, blocks_ref, *refs):
        ins, outs = refs[:rows], refs[rows:]
        here_row, here_col = lax.axis_index("prow"), lax.axis_index("pcol")
        for step in range(cols):
            q = partner(here_col, step, cols)
            total = None
            for back in range(rows):
                a = source(here_row, back, rows)
                term = jnp.dot(blocks_ref[q * rows + a], ins[back][...], preferred_element_type=F32)
                term = term * weight_ref[q * rows + a]
                total = term if total is None else total + term
            outs[step][...] = total.astype(BF16)

    return call(
        body,
        [((size, width), BF16)] * cols,
        [SMEM, VMEM] + [VMEM] * rows,
        [weights, blocks] + list(fields),
        "forward_products",
        2 * rows * cols * size * size * width,
    )


def backward_products(blocks, weights, fields, rows, cols):
    width, size = fields[0].shape

    def body(weight_ref, blocks_ref, *refs):
        ins, outs = refs[:cols], refs[cols:]
        here_row, here_col = lax.axis_index("prow"), lax.axis_index("pcol")
        for step in range(rows):
            a = partner(here_row, step, rows)
            total = None
            for back in range(cols):
                q = source(here_col, back, cols)
                term = jnp.dot(ins[back][...], blocks_ref[q * rows + a], preferred_element_type=F32)
                term = term * weight_ref[q * rows + a]
                total = term if total is None else total + term
            outs[step][...] = total.astype(BF16)

    return call(
        body,
        [((width, size), BF16)] * rows,
        [SMEM, VMEM] + [VMEM] * cols,
        [weights, blocks] + list(fields),
        "backward_products",
        2 * rows * cols * size * size * width,
    )


def shards(
    factor,
    factor_scale,
    sub_pattern,
    coupling,
    coupling_scale,
    top_pattern,
    diag_inverse,
    top_inverse,
    rhs_sub,
    rhs_top,
):
    size = factor.shape[5]
    cols = factor.shape[2]
    rows = factor.shape[3]
    layers = lax.axis_size("layer")
    width = rhs_sub.shape[-1]
    chunk = width // CHUNKS
    blocks = factor.reshape(rows * cols, size, size)
    links = coupling.reshape(rows * cols, size, size)
    weights = (factor_scale * sub_pattern.astype(F32)).reshape(rows * cols)
    link_weights = (coupling_scale * top_pattern.astype(F32)).reshape(rows * cols)
    inverse = diag_inverse.reshape(size, size)
    top_matrix = top_inverse.reshape(size, size)
    own_rhs = rhs_sub.reshape(size, width)
    top_rhs = rhs_top.reshape(size, width)
    solve_flops = 12 * size * size * chunk

    def window(index):
        return slice(index * chunk, (index + 1) * chunk)

    def begin(index):
        def body(inv_ref, rhs_ref, out_ref):
            out_ref[...] = solve_dot(inv_ref[...], rhs_ref[:, window(index)]).astype(BF16)

        return call(body, [((size, chunk), BF16)], [VMEM] * 2, [inverse, own_rhs], "begin", solve_flops)[0]

    def forward_solve(index, parts):
        def body(inv_ref, rhs_ref, *refs):
            lower = total_of(refs[:-1])
            refs[-1][...] = solve_dot(inv_ref[...], rhs_ref[:, window(index)] - lower).astype(BF16)

        return call(
            body,
            [((size, chunk), BF16)],
            [VMEM] * (2 + cols),
            [inverse, own_rhs] + list(parts),
            "forward_solve",
            solve_flops,
        )[0]

    def forward_last(index, parts):
        def body(inv_ref, rhs_ref, *refs):
            lower = total_of(refs[:-2])
            solved = solve_dot(inv_ref[...], rhs_ref[:, window(index)] - lower)
            refs[-2][...] = solved.astype(BF16)
            refs[-1][...] = solved.T

        return call(
            body,
            [((size, chunk), BF16), ((chunk, size), F32)],
            [VMEM] * (2 + cols),
            [inverse, own_rhs] + list(parts),
            "forward_last",
            solve_flops,
        )

    def top_sum(parts):
        def body(*refs):
            refs[-1][...] = total_of(refs[:-1])

        return call(body, [((size, chunk), F32)], [VMEM] * cols, list(parts), "top_sum", size * chunk)[0]

    def top_solve(index, sums):
        def body(top_ref, rhs_ref, *refs):
            merged = total_of(refs[:-2])
            half = solve_dot(top_ref[...], rhs_ref[:, window(index)] - merged)
            answer_t = solve_dot(half.T, top_ref[...])
            refs[-2][...] = answer_t.T
            refs[-1][...] = answer_t.astype(BF16)

        return call(
            body,
            [((size, chunk), F32), ((chunk, size), BF16)],
            [VMEM] * (2 + layers),
            [top_matrix, top_rhs] + list(sums),
            "top_solve",
            2 * solve_flops,
        )

    def backward_first(solved_t, parts):
        def body(inv_ref, solved_ref, *refs):
            known = solved_ref[...] - total_of(refs[:-2])
            refs[-2][...] = known
            refs[-1][...] = solve_dot(known, inv_ref[...]).astype(BF16)

        return call(
            body,
            [((chunk, size), F32), ((chunk, size), BF16)],
            [VMEM] * (2 + rows),
            [inverse, solved_t] + list(parts),
            "backward_first",
            solve_flops,
        )

    def backward_solve(known, parts):
        def body(inv_ref, known_ref, *refs):
            upper = total_of(refs[:-1])
            refs[-1][...] = solve_dot(known_ref[...] - upper, inv_ref[...]).astype(BF16)

        return call(
            body,
            [((chunk, size), BF16)],
            [VMEM] * (2 + rows),
            [inverse, known] + list(parts),
            "backward_solve",
            solve_flops,
        )[0]

    def backward_last(known, parts):
        def body(inv_ref, known_ref, *refs):
            upper = total_of(refs[:-1])
            refs[-1][...] = solve_dot(known_ref[...] - upper, inv_ref[...]).T

        return call(
            body,
            [((size, chunk), F32)],
            [VMEM] * (2 + rows),
            [inverse, known] + list(parts),
            "backward_last",
            solve_flops,
        )[0]

    group = range(CHUNKS)
    field = [begin(i) for i in group]
    solved_t = [None] * CHUNKS
    for sweep in range(LEVELS - 1):
        for i in group:
            gathered = spread(field[i], "prow", rows)
            sums = forward_products(blocks, weights, gathered, rows, cols)
            parts = exchange(sums, "pcol", cols)
            if sweep < LEVELS - 2:
                field[i] = forward_solve(i, parts)
            else:
                field[i], solved_t[i] = forward_last(i, parts)
    top_answer = [None] * CHUNKS
    for i in group:
        gathered = spread(field[i], "prow", rows)
        sums = forward_products(links, link_weights, gathered, rows, cols)
        part = top_sum(exchange(sums, "pcol", cols))
        top_answer[i], field[i] = top_solve(i, spread(part, "layer", layers))
    known = [None] * CHUNKS
    for i in group:
        gathered = spread(field[i], "pcol", cols)
        sums = backward_products(links, link_weights, gathered, rows, cols)
        known[i], field[i] = backward_first(solved_t[i], exchange(sums, "prow", rows))
    for sweep in range(LEVELS - 1):
        for i in group:
            gathered = spread(field[i], "pcol", cols)
            sums = backward_products(blocks, weights, gathered, rows, cols)
            parts = exchange(sums, "prow", rows)
            finish = backward_solve if sweep < LEVELS - 2 else backward_last
            field[i] = finish(known[i], parts)
    answer = jnp.concatenate(field, axis=1)
    top = jnp.concatenate(top_answer, axis=1)
    return answer.reshape(rhs_sub.shape), top.reshape(rhs_top.shape)


def solution(mesh):
    blocked = P("layer", "prow", None, None, "pcol", None, None)
    scales = P("layer", "prow", None, None, "pcol")
    lower = P("layer", "prow", "pcol", None, None)
    upper = P("prow", "pcol", None, None)
    return jax.shard_map(
        shards,
        mesh=mesh,
        in_specs=(blocked, scales, scales, blocked, scales, scales, lower, upper, lower, upper),
        out_specs=(lower, upper),
        check_vma=False,
    )
```

time: 299 us -> 140 us (0.47)
  waiting for transfers between devices: 159 us -> 14.1 us
  starting transfers between devices: 0.29 us -> 97.5 us
  blocking collectives: 86.8 us -> 0 us
  matrix products: 25.1 us -> 0 us
  Pallas kernels: 0 us -> 19.9 us
  between operations: 14.2 us -> 1.04 us
  local copies, waits for them, and re-layouts: 11.8 us -> 5.29 us
    ppermute x0 -> x74, starting transfers between devices: none -> 97.5 us  [exchange(): received[step] = lax.ppermute(values[step], axis, pairs)]
    all_gather x6 -> x0, blocking collectives: 86.8 us -> none  [the longest x3 48.2 us: forward_partial(): lax.all_gather(shared, 'prow', axis=0, tiled=True)]
    unnamed x10 -> x0, waiting for transfers between devices: 78.9 us -> none
    reduce_scatter x3 -> x0, waiting for transfers between devices: 59.9 us -> none  [column_total(): lax.psum_scatter(partial_value.astype(jnp.bfloat16), 'prow', scatter_dime...]
    dot_general x14 -> x0, matrix products: 25.1 us -> none  [the longest x3 8.74 us: column_total(): jnp.einsum('bakw,bkr->bawr', matrices, lax.all_gather(shared, 'pcol', axi...]
    psum x1 -> x0, waiting for transfers between devices: 20.1 us -> none  [shards(): lax.psum(top_part.astype(jnp.bfloat16), 'layer').astype(jnp.float32)]
    pallas_call x0 -> x28, Pallas kernels: none -> 19.9 us  [call(): pl.pallas_call(body, out_shape=[jax.ShapeDtypeStruct(shape, dtype) for sh...]
    ppermute x0 -> x74, waiting for transfers between devices: none -> 14.1 us  [exchange(): received[step] = lax.ppermute(values[step], axis, pairs)]
  transfers between devices with their start and end apart: 7 -> 74, of which waited for: 7 -> 7; matrix products, arithmetic and copies ran while one was open for 0% -> 1% of each run, Pallas kernels for 0% -> 14%
where the time goes in v1:
time: 140 us
  starting transfers between devices  97.5 us (70%)
  Pallas kernels  19.9 us (14%)
  waiting for transfers between devices  14.1 us (10%)
  local copies, waits for them, and re-layouts  5.29 us (4%)
  other arithmetic  2.19 us (2%)
    ppermute x74, starting transfers between devices, exchange(): received[step] = lax.ppermute(values[step], axis, pairs)  97.5 us
    pallas_call x28, Pallas kernels, call(): pl.pallas_call(body, out_shape=[jax.ShapeDtypeStruct(shape, dtype) for sh...  19.9 us
    ppermute x74, waiting for transfers between devices, exchange(): received[step] = lax.ppermute(values[step], axis, pairs)  14.1 us
    unnamed x24, local copies, waits for them, and re-layouts  5.12 us
  transfers between devices with their start and end apart: 74, of which 7 were waited for; matrix products, arithmetic and copies ran while one was open for 1% of the time, Pallas kernels for 14%

profile of v1, /device:TPU:0, one launch (start us, length us, event | category | flops | bytes accessed | tf_op | source)
XLA Modules:
  0.0 140.0 jit_solution(3660897614160346388)
XLA Ops:
  2.9 5.1 %collective-permute-start.39 = (bf16[256,128]{1,0:T(8,128)(2,1)S(1)}, bf16[256,128]{1,0:T(8,128)(2,1)S(1)}, u32[]{:S(2)}, u32[]{:S(2)}) collective-permute-start(bf16[256,128]{1,0:T(8,128)(2,1)S(1)} %begin.3.refs_0_), channel_id=1, source_target_pairs={{0,12},{4,8},{8,4},{12,0},{1,13},{5,9},{9,5},{13,1},{2,14},{6,10},... | collective-permute-start | bytes 196616 | tf_op jit(solution)/shard_map/ppermute | solution.py:38
  8.5 1.0 collective-permute-start.1
  9.5 3.4 %collective-permute-start = (bf16[256,128]{1,0:T(8,128)(2,1)S(1)}, bf16[256,128]{1,0:T(8,128)(2,1)S(1)}, u32[]{:S(2)}, u32[]{:S(2)}) collective-permute-start(bf16[256,128]{1,0:T(8,128)(2,1)S(1)} %begin.2.refs_0_), channel_id=1, source_target_pairs={{0,4},{4,0},{8,12},{12,8},{1,5},{5,1},{9,13},{13,9},{2,6},{6,2},{1... | collective-permute-start | bytes 196616 | tf_op jit(solution)/shard_map/ppermute | solution.py:38
  14.3 5.0 %collective-permute-done.38.refs_2_ = bf16[256,128]{1,0:T(8,128)(2,1)S(1)} collective-permute-done((bf16[256,128]{1,0:T(8,128)(2,1)S(1)}, bf16[256,128]{1,0:T(8,128)(2,1)S(1)}, u32[]{:S(2)}, u32[]{:S(2)}) %collective-permute-start.38) | collective-permute-done | bytes 65568 | tf_op jit(solution)/shard_map/ppermute | solution.py:38
  19.3 1.6 %copy-done = bf16[1,1,4,4,1,256,256]{6,5,4,3,2,1,0:T(8,128)(2,1)S(1)} copy-done((bf16[1,1,4,4,1,256,256]{6,5,4,3,2,1,0:T(8,128)(2,1)S(1)}, bf16[1,1,4,4,1,256,256]{6,5,4,3,2,1,0:T(8,128)(2,1)}, u32[]{:S(2)}) %copy-start) | copy-done | bytes 2097176
  20.9 1.2 forward_products.9
  22.2 1.6 %collective-permute-start.40 = (bf16[256,128]{1,0:T(8,128)(2,1)S(1)}, bf16[256,128]{1,0:T(8,128)(2,1)S(1)}, u32[]{:S(2)}, u32[]{:S(2)}) collective-permute-start(bf16[256,128]{1,0:T(8,128)(2,1)S(1)} %get-tuple-element.92), channel_id=1, source_target_pairs={{0,1},{1,0},{2,3},{3,2},{4,5},{5,4},{6,7},{7,6},{8,9},{9,8},{10,11... | collective-permute-start | bytes 196616 | tf_op jit(solution)/shard_map/ppermute | solution.py:38
  23.7 1.5 %collective-permute-start.41 = (bf16[256,128]{1,0:T(8,128)(2,1)S(1)}, bf16[256,128]{1,0:T(8,128)(2,1)S(1)}, u32[]{:S(2)}, u32[]{:S(2)}) collective-permute-start(bf16[256,128]{1,0:T(8,128)(2,1)S(1)} %get-tuple-element.93), channel_id=1, source_target_pairs={{0,2},{1,3},{2,0},{3,1},{4,6},{5,7},{6,4},{7,5},{8,10},{9,11},{10,... | collective-permute-start | bytes 196616 | tf_op jit(solution)/shard_map/ppermute | solution.py:38
  25.7 1.2 forward_products.6
  27.0 1.6 %collective-permute-start.3 = (bf16[256,128]{1,0:T(8,128)(2,1)S(1)}, bf16[256,128]{1,0:T(8,128)(2,1)S(1)}, u32[]{:S(2)}, u32[]{:S(2)}) collective-permute-start(bf16[256,128]{1,0:T(8,128)(2,1)S(1)} %get-tuple-element.63), channel_id=1, source_target_pairs={{0,1},{1,0},{2,3},{3,2},{4,5},{5,4},{6,7},{7,6},{8,9},{9,8},{10,11... | collective-permute-start | bytes 196616 | tf_op jit(solution)/shard_map/ppermute | solution.py:38
  28.6 1.5 %collective-permute-start.4 = (bf16[256,128]{1,0:T(8,128)(2,1)S(1)}, bf16[256,128]{1,0:T(8,128)(2,1)S(1)}, u32[]{:S(2)}, u32[]{:S(2)}) collective-permute-start(bf16[256,128]{1,0:T(8,128)(2,1)S(1)} %get-tuple-element.64), channel_id=1, source_target_pairs={{0,2},{1,3},{2,0},{3,1},{4,6},{5,7},{6,4},{7,5},{8,10},{9,11},{10,... | collective-permute-start | bytes 196616 | tf_op jit(solution)/shard_map/ppermute | solution.py:38
  31.0 2.4 %collective-permute-start.45 = (bf16[256,128]{1,0:T(8,128)(2,1)S(1)}, bf16[256,128]{1,0:T(8,128)(2,1)S(1)}, u32[]{:S(2)}, u32[]{:S(2)}) collective-permute-start(bf16[256,128]{1,0:T(8,128)(2,1)S(1)} %forward_solve.3.refs_0_), channel_id=1, source_target_pairs={{0,12},{4,8},{8,4},{12,0},{1,13},{5,9},{9,5},{13,1},{2,14},{6,10},... | collective-permute-start | bytes 196616 | tf_op jit(solution)/shard_map/ppermute | solution.py:38
  33.3 2.1 %collective-permute-start.43 = (bf16[256,128]{1,0:T(8,128)(2,1)S(1)}, bf16[256,128]{1,0:T(8,128)(2,1)S(1)}, u32[]{:S(2)}, u32[]{:S(2)}) collective-permute-start(bf16[256,128]{1,0:T(8,128)(2,1)S(1)} %forward_solve.3.refs_0_), channel_id=1, source_target_pairs={{0,4},{4,0},{8,12},{12,8},{1,5},{5,1},{9,13},{13,9},{2,6},{6,2},{1... | collective-permute-start | bytes 196616 | tf_op jit(solution)/shard_map/ppermute | solution.py:38
  35.8 2.4 %collective-permute-start.8 = (bf16[256,128]{1,0:T(8,128)(2,1)S(1)}, bf16[256,128]{1,0:T(8,128)(2,1)S(1)}, u32[]{:S(2)}, u32[]{:S(2)}) collective-permute-start(bf16[256,128]{1,0:T(8,128)(2,1)S(1)} %forward_solve.2.refs_0_), channel_id=1, source_target_pairs={{0,12},{4,8},{8,4},{12,0},{1,13},{5,9},{9,5},{13,1},{2,14},{6,10},... | collective-permute-start | bytes 196616 | tf_op jit(solution)/shard_map/ppermute | solution.py:38
  38.2 2.1 %collective-permute-start.6 = (bf16[256,128]{1,0:T(8,128)(2,1)S(1)}, bf16[256,128]{1,0:T(8,128)(2,1)S(1)}, u32[]{:S(2)}, u32[]{:S(2)}) collective-permute-start(bf16[256,128]{1,0:T(8,128)(2,1)S(1)} %forward_solve.2.refs_0_), channel_id=1, source_target_pairs={{0,4},{4,0},{8,12},{12,8},{1,5},{5,1},{9,13},{13,9},{2,6},{6,2},{1... | collective-permute-start | bytes 196616 | tf_op jit(solution)/shard_map/ppermute | solution.py:38
  40.6 1.2 forward_products.10
  41.9 1.5 %collective-permute-start.46 = (bf16[256,128]{1,0:T(8,128)(2,1)S(1)}, bf16[256,128]{1,0:T(8,128)(2,1)S(1)}, u32[]{:S(2)}, u32[]{:S(2)}) collective-permute-start(bf16[256,128]{1,0:T(8,128)(2,1)S(1)} %get-tuple-element.96), channel_id=1, source_target_pairs={{0,1},{1,0},{2,3},{3,2},{4,5},{5,4},{6,7},{7,6},{8,9},{9,8},{10,11... | collective-permute-start | bytes 196616 | tf_op jit(solution)/shard_map/ppermute | solution.py:38
  43.4 1.5 %collective-permute-start.47 = (bf16[256,128]{1,0:T(8,128)(2,1)S(1)}, bf16[256,128]{1,0:T(8,128)(2,1)S(1)}, u32[]{:S(2)}, u32[]{:S(2)}) collective-permute-start(bf16[256,128]{1,0:T(8,128)(2,1)S(1)} %get-tuple-element.97), channel_id=1, source_target_pairs={{0,2},{1,3},{2,0},{3,1},{4,6},{5,7},{6,4},{7,5},{8,10},{9,11},{10,... | collective-permute-start | bytes 196616 | tf_op jit(solution)/shard_map/ppermute | solution.py:38
  45.5 1.2 forward_products.7
  46.7 1.5 %collective-permute-start.9 = (bf16[256,128]{1,0:T(8,128)(2,1)S(1)}, bf16[256,128]{1,0:T(8,128)(2,1)S(1)}, u32[]{:S(2)}, u32[]{:S(2)}) collective-permute-start(bf16[256,128]{1,0:T(8,128)(2,1)S(1)} %get-tuple-element.67), channel_id=1, source_target_pairs={{0,1},{1,0},{2,3},{3,2},{4,5},{5,4},{6,7},{7,6},{8,9},{9,8},{10,11... | collective-permute-start | bytes 196616 | tf_op jit(solution)/shard_map/ppermute | solution.py:38
  48.2 1.5 %collective-permute-start.10 = (bf16[256,128]{1,0:T(8,128)(2,1)S(1)}, bf16[256,128]{1,0:T(8,128)(2,1)S(1)}, u32[]{:S(2)}, u32[]{:S(2)}) collective-permute-start(bf16[256,128]{1,0:T(8,128)(2,1)S(1)} %get-tuple-element.68), channel_id=1, source_target_pairs={{0,2},{1,3},{2,0},{3,1},{4,6},{5,7},{6,4},{7,5},{8,10},{9,11},{10,... | collective-permute-start | bytes 196616 | tf_op jit(solution)/shard_map/ppermute | solution.py:38
  50.7 2.5 %collective-permute-start.51 = (bf16[256,128]{1,0:T(8,128)(2,1)S(1)}, bf16[256,128]{1,0:T(8,128)(2,1)S(1)}, u32[]{:S(2)}, u32[]{:S(2)}) collective-permute-start(bf16[256,128]{1,0:T(8,128)(2,1)S(1)} %get-tuple-element.100.refs_0_), channel_id=1, source_target_pairs={{0,12},{4,8},{8,4},{12,0},{1,13},{5,9},{9,5},{13,1},{2,14},{6,10},... | collective-permute-start | bytes 196616 | tf_op jit(solution)/shard_map/ppermute | solution.py:38
  53.2 2.0 %collective-permute-start.49 = (bf16[256,128]{1,0:T(8,128)(2,1)S(1)}, bf16[256,128]{1,0:T(8,128)(2,1)S(1)}, u32[]{:S(2)}, u32[]{:S(2)}) collective-permute-start(bf16[256,128]{1,0:T(8,128)(2,1)S(1)} %get-tuple-element.100.refs_0_), channel_id=1, source_target_pairs={{0,4},{4,0},{8,12},{12,8},{1,5},{5,1},{9,13},{13,9},{2,6},{6,2},{1... | collective-permute-start | bytes 196616 | tf_op jit(solution)/shard_map/ppermute | solution.py:38
  55.6 2.5 %collective-permute-start.14 = (bf16[256,128]{1,0:T(8,128)(2,1)S(1)}, bf16[256,128]{1,0:T(8,128)(2,1)S(1)}, u32[]{:S(2)}, u32[]{:S(2)}) collective-permute-start(bf16[256,128]{1,0:T(8,128)(2,1)S(1)} %get-tuple-element.71.refs_0_), channel_id=1, source_target_pairs={{0,12},{4,8},{8,4},{12,0},{1,13},{5,9},{9,5},{13,1},{2,14},{6,10},... | collective-permute-start | bytes 196616 | tf_op jit(solution)/shard_map/ppermute | solution.py:38
  58.2 2.0 %collective-permute-start.12 = (bf16[256,128]{1,0:T(8,128)(2,1)S(1)}, bf16[256,128]{1,0:T(8,128)(2,1)S(1)}, u32[]{:S(2)}, u32[]{:S(2)}) collective-permute-start(bf16[256,128]{1,0:T(8,128)(2,1)S(1)} %get-tuple-element.71.refs_0_), channel_id=1, source_target_pairs={{0,4},{4,0},{8,12},{12,8},{1,5},{5,1},{9,13},{13,9},{2,6},{6,2},{1... | collective-permute-start | bytes 196616 | tf_op jit(solution)/shard_map/ppermute | solution.py:38
  60.2 1.6 %copy-done.4 = bf16[1,1,4,4,1,256,256]{6,5,4,3,2,1,0:T(8,128)(2,1)S(1)} copy-done((bf16[1,1,4,4,1,256,256]{6,5,4,3,2,1,0:T(8,128)(2,1)S(1)}, bf16[1,1,4,4,1,256,256]{6,5,4,3,2,1,0:T(8,128)(2,1)}, u32[]{:S(2)}) %copy-start.4) | copy-done | bytes 2097176
  61.8 1.2 forward_products.11
  63.1 1.5 %collective-permute-start.52 = (bf16[256,128]{1,0:T(8,128)(2,1)S(1)}, bf16[256,128]{1,0:T(8,128)(2,1)S(1)}, u32[]{:S(2)}, u32[]{:S(2)}) collective-permute-start(bf16[256,128]{1,0:T(8,128)(2,1)S(1)} %get-tuple-element.102), channel_id=1, source_target_pairs={{0,1},{1,0},{2,3},{3,2},{4,5},{5,4},{6,7},{7,6},{8,9},{9,8},{10,11... | collective-permute-start | bytes 196616 | tf_op jit(solution)/shard_map/ppermute | solution.py:38
  64.6 1.5 %collective-permute-start.53 = (bf16[256,128]{1,0:T(8,128)(2,1)S(1)}, bf16[256,128]{1,0:T(8,128)(2,1)S(1)}, u32[]{:S(2)}, u32[]{:S(2)}) collective-permute-start(bf16[256,128]{1,0:T(8,128)(2,1)S(1)} %get-tuple-element.103), channel_id=1, source_target_pairs={{0,2},{1,3},{2,0},{3,1},{4,6},{5,7},{6,4},{7,5},{8,10},{9,11},{10,... | collective-permute-start | bytes 196616 | tf_op jit(solution)/shard_map/ppermute | solution.py:38
  66.7 1.2 forward_products.8
  67.9 1.5 %collective-permute-start.15 = (bf16[256,128]{1,0:T(8,128)(2,1)S(1)}, bf16[256,128]{1,0:T(8,128)(2,1)S(1)}, u32[]{:S(2)}, u32[]{:S(2)}) collective-permute-start(bf16[256,128]{1,0:T(8,128)(2,1)S(1)} %get-tuple-element.73), channel_id=1, source_target_pairs={{0,1},{1,0},{2,3},{3,2},{4,5},{5,4},{6,7},{7,6},{8,9},{9,8},{10,11... | collective-permute-start | bytes 196616 | tf_op jit(solution)/shard_map/ppermute | solution.py:38
  69.4 1.5 %collective-permute-start.16 = (bf16[256,128]{1,0:T(8,128)(2,1)S(1)}, bf16[256,128]{1,0:T(8,128)(2,1)S(1)}, u32[]{:S(2)}, u32[]{:S(2)}) collective-permute-start(bf16[256,128]{1,0:T(8,128)(2,1)S(1)} %get-tuple-element.74), channel_id=1, source_target_pairs={{0,2},{1,3},{2,0},{3,1},{4,6},{5,7},{6,4},{7,5},{8,10},{9,11},{10,... | collective-permute-start | bytes 196616 | tf_op jit(solution)/shard_map/ppermute | solution.py:38
  72.2 1.4 %collective-permute-done.16.refs_2_ = bf16[256,128]{1,0:T(8,128)(2,1)S(1)} collective-permute-done((bf16[256,128]{1,0:T(8,128)(2,1)S(1)}, bf16[256,128]{1,0:T(8,128)(2,1)S(1)}, u32[]{:S(2)}, u32[]{:S(2)}) %collective-permute-start.16) | collective-permute-done | bytes 65568 | tf_op jit(solution)/shard_map/ppermute | solution.py:38
  73.7 2.4 %collective-permute-done.17.refs_3_ = bf16[256,128]{1,0:T(8,128)(2,1)S(1)} collective-permute-done((bf16[256,128]{1,0:T(8,128)(2,1)S(1)}, bf16[256,128]{1,0:T(8,128)(2,1)S(1)}, u32[]{:S(2)}, u32[]{:S(2)}) %collective-permute-start.17) | collective-permute-done | bytes 65568 | tf_op jit(solution)/shard_map/ppermute | solution.py:38
  77.7 1.5 %collective-permute-start.57 = (bf16[128,256]{1,0:T(8,128)(2,1)S(1)}, bf16[128,256]{1,0:T(8,128)(2,1)S(1)}, u32[]{:S(2)}, u32[]{:S(2)}) collective-permute-start(bf16[128,256]{1,0:T(8,128)(2,1)S(1)} %get-tuple-element.105.refs_0_), channel_id=1, source_target_pairs={{0,2},{1,3},{2,0},{3,1},{4,6},{5,7},{6,4},{7,5},{8,10},{9,11},{10,... | collective-permute-start | bytes 196616 | tf_op jit(solution)/shard_map/ppermute | solution.py:38
  79.2 1.5 %collective-permute-start.56 = (bf16[128,256]{1,0:T(8,128)(2,1)S(1)}, bf16[128,256]{1,0:T(8,128)(2,1)S(1)}, u32[]{:S(2)}, u32[]{:S(2)}) collective-permute-start(bf16[128,256]{1,0:T(8,128)(2,1)S(1)} %get-tuple-element.105.refs_0_), channel_id=1, source_target_pairs={{0,1},{1,0},{2,3},{3,2},{4,5},{5,4},{6,7},{7,6},{8,9},{9,8},{10,11... | collective-permute-start | bytes 196616 | tf_op jit(solution)/shard_map/ppermute | solution.py:38
  82.2 1.5 %collective-permute-start.20 = (bf16[128,256]{1,0:T(8,128)(2,1)S(1)}, bf16[128,256]{1,0:T(8,128)(2,1)S(1)}, u32[]{:S(2)}, u32[]{:S(2)}) collective-permute-start(bf16[128,256]{1,0:T(8,128)(2,1)S(1)} %get-tuple-element.76.refs_0_), channel_id=1, source_target_pairs={{0,2},{1,3},{2,0},{3,1},{4,6},{5,7},{6,4},{7,5},{8,10},{9,11},{10,... | collective-permute-start | bytes 196616 | tf_op jit(solution)/shard_map/ppermute | solution.py:38
  83.7 1.5 %collective-permute-start.19 = (bf16[128,256]{1,0:T(8,128)(2,1)S(1)}, bf16[128,256]{1,0:T(8,128)(2,1)S(1)}, u32[]{:S(2)}, u32[]{:S(2)}) collective-permute-start(bf16[128,256]{1,0:T(8,128)(2,1)S(1)} %get-tuple-element.76.refs_0_), channel_id=1, source_target_pairs={{0,1},{1,0},{2,3},{3,2},{4,5},{5,4},{6,7},{7,6},{8,9},{9,8},{10,11... | collective-permute-start | bytes 196616 | tf_op jit(solution)/shard_map/ppermute | solution.py:38
  86.4 2.8 %collective-permute-start.60 = (bf16[128,256]{1,0:T(8,128)(2,1)S(1)}, bf16[128,256]{1,0:T(8,128)(2,1)S(1)}, u32[]{:S(2)}, u32[]{:S(2)}) collective-permute-start(bf16[128,256]{1,0:T(8,128)(2,1)S(1)} %get-tuple-element.108), channel_id=1, source_target_pairs={{0,8},{4,12},{8,0},{12,4},{1,9},{5,13},{9,1},{13,5},{2,10},{6,14},... | collective-permute-start | bytes 196616 | tf_op jit(solution)/shard_map/ppermute | solution.py:38
  89.2 1.4 %collective-permute-start.61 = (bf16[128,256]{1,0:T(8,128)(2,1)S(1)}, bf16[128,256]{1,0:T(8,128)(2,1)S(1)}, u32[]{:S(2)}, u32[]{:S(2)}) collective-permute-start(bf16[128,256]{1,0:T(8,128)(2,1)S(1)} %get-tuple-element.109), channel_id=1, source_target_pairs={{0,12},{4,8},{8,4},{12,0},{1,13},{5,9},{9,5},{13,1},{2,14},{6,10},... | collective-permute-start | bytes 196616 | tf_op jit(solution)/shard_map/ppermute | solution.py:38
  90.6 1.2 backward_products.6
  91.9 3.0 %collective-permute-start.23 = (bf16[128,256]{1,0:T(8,128)(2,1)S(1)}, bf16[128,256]{1,0:T(8,128)(2,1)S(1)}, u32[]{:S(2)}, u32[]{:S(2)}) collective-permute-start(bf16[128,256]{1,0:T(8,128)(2,1)S(1)} %get-tuple-element.79), channel_id=1, source_target_pairs={{0,8},{4,12},{8,0},{12,4},{1,9},{5,13},{9,1},{13,5},{2,10},{6,14},... | collective-permute-start | bytes 196616 | tf_op jit(solution)/shard_map/ppermute | solution.py:38
  94.9 1.4 %collective-permute-start.24 = (bf16[128,256]{1,0:T(8,128)(2,1)S(1)}, bf16[128,256]{1,0:T(8,128)(2,1)S(1)}, u32[]{:S(2)}, u32[]{:S(2)}) collective-permute-start(bf16[128,256]{1,0:T(8,128)(2,1)S(1)} %get-tuple-element.80), channel_id=1, source_target_pairs={{0,12},{4,8},{8,4},{12,0},{1,13},{5,9},{9,5},{13,1},{2,14},{6,10},... | collective-permute-start | bytes 196616 | tf_op jit(solution)/shard_map/ppermute | solution.py:38
  97.2 1.5 %collective-permute-start.63 = (bf16[128,256]{1,0:T(8,128)(2,1)S(1)}, bf16[128,256]{1,0:T(8,128)(2,1)S(1)}, u32[]{:S(2)}, u32[]{:S(2)}) collective-permute-start(bf16[128,256]{1,0:T(8,128)(2,1)S(1)} %get-tuple-element.111.refs_0_), channel_id=1, source_target_pairs={{0,2},{1,3},{2,0},{3,1},{4,6},{5,7},{6,4},{7,5},{8,10},{9,11},{10,... | collective-permute-start | bytes 196616 | tf_op jit(solution)/shard_map/ppermute | solution.py:38
  98.7 1.5 %collective-permute-start.62 = (bf16[128,256]{1,0:T(8,128)(2,1)S(1)}, bf16[128,256]{1,0:T(8,128)(2,1)S(1)}, u32[]{:S(2)}, u32[]{:S(2)}) collective-permute-start(bf16[128,256]{1,0:T(8,128)(2,1)S(1)} %get-tuple-element.111.refs_0_), channel_id=1, source_target_pairs={{0,1},{1,0},{2,3},{3,2},{4,5},{5,4},{6,7},{7,6},{8,9},{9,8},{10,11... | collective-permute-start | bytes 196616 | tf_op jit(solution)/shard_map/ppermute | solution.py:38
  101.8 1.5 %collective-permute-start.26 = (bf16[128,256]{1,0:T(8,128)(2,1)S(1)}, bf16[128,256]{1,0:T(8,128)(2,1)S(1)}, u32[]{:S(2)}, u32[]{:S(2)}) collective-permute-start(bf16[128,256]{1,0:T(8,128)(2,1)S(1)} %get-tuple-element.82.refs_0_), channel_id=1, source_target_pairs={{0,2},{1,3},{2,0},{3,1},{4,6},{5,7},{6,4},{7,5},{8,10},{9,11},{10,... | collective-permute-start | bytes 196616 | tf_op jit(solution)/shard_map/ppermute | solution.py:38
  103.3 1.5 %collective-permute-start.25 = (bf16[128,256]{1,0:T(8,128)(2,1)S(1)}, bf16[128,256]{1,0:T(8,128)(2,1)S(1)}, u32[]{:S(2)}, u32[]{:S(2)}) collective-permute-start(bf16[128,256]{1,0:T(8,128)(2,1)S(1)} %get-tuple-element.82.refs_0_), channel_id=1, source_target_pairs={{0,1},{1,0},{2,3},{3,2},{4,5},{5,4},{6,7},{7,6},{8,9},{9,8},{10,11... | collective-permute-start | bytes 196616 | tf_op jit(solution)/shard_map/ppermute | solution.py:38
  104.8 1.0 backward_products.10
  105.9 2.2 %collective-permute-start.66 = (bf16[128,256]{1,0:T(8,128)(2,1)S(1)}, bf16[128,256]{1,0:T(8,128)(2,1)S(1)}, u32[]{:S(2)}, u32[]{:S(2)}) collective-permute-start(bf16[128,256]{1,0:T(8,128)(2,1)S(1)} %get-tuple-element.114), channel_id=1, source_target_pairs={{0,8},{4,12},{8,0},{12,4},{1,9},{5,13},{9,1},{13,5},{2,10},{6,14},... | collective-permute-start | bytes 196616 | tf_op jit(solution)/shard_map/ppermute | solution.py:38
  108.1 2.2 %collective-permute-start.67 = (bf16[128,256]{1,0:T(8,128)(2,1)S(1)}, bf16[128,256]{1,0:T(8,128)(2,1)S(1)}, u32[]{:S(2)}, u32[]{:S(2)}) collective-permute-start(bf16[128,256]{1,0:T(8,128)(2,1)S(1)} %get-tuple-element.115), channel_id=1, source_target_pairs={{0,12},{4,8},{8,4},{12,0},{1,13},{5,9},{9,5},{13,1},{2,14},{6,10},... | collective-permute-start | bytes 196616 | tf_op jit(solution)/shard_map/ppermute | solution.py:38
  110.3 1.0 backward_products.7
  111.4 2.2 %collective-permute-start.29 = (bf16[128,256]{1,0:T(8,128)(2,1)S(1)}, bf16[128,256]{1,0:T(8,128)(2,1)S(1)}, u32[]{:S(2)}, u32[]{:S(2)}) collective-permute-start(bf16[128,256]{1,0:T(8,128)(2,1)S(1)} %get-tuple-element.85), channel_id=1, source_target_pairs={{0,8},{4,12},{8,0},{12,4},{1,9},{5,13},{9,1},{13,5},{2,10},{6,14},... | collective-permute-start | bytes 196616 | tf_op jit(solution)/shard_map/ppermute | solution.py:38
  113.6 2.2 %collective-permute-start.30 = (bf16[128,256]{1,0:T(8,128)(2,1)S(1)}, bf16[128,256]{1,0:T(8,128)(2,1)S(1)}, u32[]{:S(2)}, u32[]{:S(2)}) collective-permute-start(bf16[128,256]{1,0:T(8,128)(2,1)S(1)} %get-tuple-element.86), channel_id=1, source_target_pairs={{0,12},{4,8},{8,4},{12,0},{1,13},{5,9},{9,5},{13,1},{2,14},{6,10},... | collective-permute-start | bytes 196616 | tf_op jit(solution)/shard_map/ppermute | solution.py:38
  116.7 1.5 %collective-permute-start.69 = (bf16[128,256]{1,0:T(8,128)(2,1)S(1)}, bf16[128,256]{1,0:T(8,128)(2,1)S(1)}, u32[]{:S(2)}, u32[]{:S(2)}) collective-permute-start(bf16[128,256]{1,0:T(8,128)(2,1)S(1)} %backward_solve.3.refs_0_), channel_id=1, source_target_pairs={{0,2},{1,3},{2,0},{3,1},{4,6},{5,7},{6,4},{7,5},{8,10},{9,11},{10,... | collective-permute-start | bytes 196616 | tf_op jit(solution)/shard_map/ppermute | solution.py:38
  118.2 1.5 %collective-permute-start.68 = (bf16[128,256]{1,0:T(8,128)(2,1)S(1)}, bf16[128,256]{1,0:T(8,128)(2,1)S(1)}, u32[]{:S(2)}, u32[]{:S(2)}) collective-permute-start(bf16[128,256]{1,0:T(8,128)(2,1)S(1)} %backward_solve.3.refs_0_), channel_id=1, source_target_pairs={{0,1},{1,0},{2,3},{3,2},{4,5},{5,4},{6,7},{7,6},{8,9},{9,8},{10,11... | collective-permute-start | bytes 196616 | tf_op jit(solution)/shard_map/ppermute | solution.py:38
  120.5 1.5 %collective-permute-start.32 = (bf16[128,256]{1,0:T(8,128)(2,1)S(1)}, bf16[128,256]{1,0:T(8,128)(2,1)S(1)}, u32[]{:S(2)}, u32[]{:S(2)}) collective-permute-start(bf16[128,256]{1,0:T(8,128)(2,1)S(1)} %backward_solve.2.refs_0_), channel_id=1, source_target_pairs={{0,2},{1,3},{2,0},{3,1},{4,6},{5,7},{6,4},{7,5},{8,10},{9,11},{10,... | collective-permute-start | bytes 196616 | tf_op jit(solution)/shard_map/ppermute | solution.py:38
  122.0 1.5 %collective-permute-start.31 = (bf16[128,256]{1,0:T(8,128)(2,1)S(1)}, bf16[128,256]{1,0:T(8,128)(2,1)S(1)}, u32[]{:S(2)}, u32[]{:S(2)}) collective-permute-start(bf16[128,256]{1,0:T(8,128)(2,1)S(1)} %backward_solve.2.refs_0_), channel_id=1, source_target_pairs={{0,1},{1,0},{2,3},{3,2},{4,5},{5,4},{6,7},{7,6},{8,9},{9,8},{10,11... | collective-permute-start | bytes 196616 | tf_op jit(solution)/shard_map/ppermute | solution.py:38
  123.5 1.0 backward_products.11
  124.7 2.7 %collective-permute-start.72 = (bf16[128,256]{1,0:T(8,128)(2,1)S(1)}, bf16[128,256]{1,0:T(8,128)(2,1)S(1)}, u32[]{:S(2)}, u32[]{:S(2)}) collective-permute-start(bf16[128,256]{1,0:T(8,128)(2,1)S(1)} %get-tuple-element.118), channel_id=1, source_target_pairs={{0,8},{4,12},{8,0},{12,4},{1,9},{5,13},{9,1},{13,5},{2,10},{6,14},... | collective-permute-start | bytes 196616 | tf_op jit(solution)/shard_map/ppermute | solution.py:38
  127.4 1.7 %collective-permute-start.73 = (bf16[128,256]{1,0:T(8,128)(2,1)S(1)}, bf16[128,256]{1,0:T(8,128)(2,1)S(1)}, u32[]{:S(2)}, u32[]{:S(2)}) collective-permute-start(bf16[128,256]{1,0:T(8,128)(2,1)S(1)} %get-tuple-element.119), channel_id=1, source_target_pairs={{0,12},{4,8},{8,4},{12,0},{1,13},{5,9},{9,5},{13,1},{2,14},{6,10},... | collective-permute-start | bytes 196616 | tf_op jit(solution)/shard_map/ppermute | solution.py:38
  129.0 1.0 backward_products.8
  130.1 2.7 %collective-permute-start.35 = (bf16[128,256]{1,0:T(8,128)(2,1)S(1)}, bf16[128,256]{1,0:T(8,128)(2,1)S(1)}, u32[]{:S(2)}, u32[]{:S(2)}) collective-permute-start(bf16[128,256]{1,0:T(8,128)(2,1)S(1)} %get-tuple-element.89), channel_id=1, source_target_pairs={{0,8},{4,12},{8,0},{12,4},{1,9},{5,13},{9,1},{13,5},{2,10},{6,14},... | collective-permute-start | bytes 196616 | tf_op jit(solution)/shard_map/ppermute | solution.py:38
  132.9 1.7 %collective-permute-start.36 = (bf16[128,256]{1,0:T(8,128)(2,1)S(1)}, bf16[128,256]{1,0:T(8,128)(2,1)S(1)}, u32[]{:S(2)}, u32[]{:S(2)}) collective-permute-start(bf16[128,256]{1,0:T(8,128)(2,1)S(1)} %get-tuple-element.90), channel_id=1, source_target_pairs={{0,12},{4,8},{8,4},{12,0},{1,13},{5,9},{9,5},{13,1},{2,14},{6,10},... | collective-permute-start | bytes 196616 | tf_op jit(solution)/shard_map/ppermute | solution.py:38
  135.7 3.3 %collective-permute-done.36.refs_3_ = bf16[128,256]{1,0:T(8,128)(2,1)S(1)} collective-permute-done((bf16[128,256]{1,0:T(8,128)(2,1)S(1)}, bf16[128,256]{1,0:T(8,128)(2,1)S(1)}, u32[]{:S(2)}, u32[]{:S(2)}) %collective-permute-start.36) | collective-permute-done | bytes 65568 | tf_op jit(solution)/shard_map/ppermute | solution.py:38
  (142 shorter events, 21.5 us)
Async XLA Ops:
  2.9 10.0 %collective-permute-start.39 = (bf16[256,128]{1,0:T(8,128)(2,1)S(1)}, bf16[256,128]{1,0:T(8,128)(2,1)S(1)}, u32[]{:S(2)}, u32[]{:S(2)}) collective-permute-start(bf16[256,128]{1,0:T(8,128)(2,1)S(1)} %begin.3.refs_0_), channel_id=1, source_target_pairs={{0,12},{4,8},{8,4},{12,0},{1,13},{5,9},{9,5},{13,1},{2,14},{6,10},... | collective-permute-start | bytes 196616 | tf_op jit(solution)/shard_map/ppermute | solution.py:38
  8.4 16.8 %collective-permute-start.2 = (bf16[256,128]{1,0:T(8,128)(2,1)S(1)}, bf16[256,128]{1,0:T(8,128)(2,1)S(1)}, u32[]{:S(2)}, u32[]{:S(2)}) collective-permute-start(bf16[256,128]{1,0:T(8,128)(2,1)S(1)} %begin.2.refs_0_), channel_id=1, source_target_pairs={{0,12},{4,8},{8,4},{12,0},{1,13},{5,9},{9,5},{13,1},{2,14},{6,10},... | collective-permute-start | bytes 196616 | tf_op jit(solution)/shard_map/ppermute | solution.py:38
  8.5 17.2 %collective-permute-start.1 = (bf16[256,128]{1,0:T(8,128)(2,1)S(1)}, bf16[256,128]{1,0:T(8,128)(2,1)S(1)}, u32[]{:S(2)}, u32[]{:S(2)}) collective-permute-start(bf16[256,128]{1,0:T(8,128)(2,1)S(1)} %begin.2.refs_0_), channel_id=1, source_target_pairs={{0,8},{4,12},{8,0},{12,4},{1,9},{5,13},{9,1},{13,5},{2,10},{6,14},... | collective-permute-start | bytes 196616 | tf_op jit(solution)/shard_map/ppermute | solution.py:38
  9.5 16.2 %collective-permute-start = (bf16[256,128]{1,0:T(8,128)(2,1)S(1)}, bf16[256,128]{1,0:T(8,128)(2,1)S(1)}, u32[]{:S(2)}, u32[]{:S(2)}) collective-permute-start(bf16[256,128]{1,0:T(8,128)(2,1)S(1)} %begin.2.refs_0_), channel_id=1, source_target_pairs={{0,4},{4,0},{8,12},{12,8},{1,5},{5,1},{9,13},{13,9},{2,6},{6,2},{1... | collective-permute-start | bytes 196616 | tf_op jit(solution)/shard_map/ppermute | solution.py:38
  12.9 6.4 %collective-permute-start.38 = (bf16[256,128]{1,0:T(8,128)(2,1)S(1)}, bf16[256,128]{1,0:T(8,128)(2,1)S(1)}, u32[]{:S(2)}, u32[]{:S(2)}) collective-permute-start(bf16[256,128]{1,0:T(8,128)(2,1)S(1)} %begin.3.refs_0_), channel_id=1, source_target_pairs={{0,8},{4,12},{8,0},{12,4},{1,9},{5,13},{9,1},{13,5},{2,10},{6,14},... | collective-permute-start | bytes 196616 | tf_op jit(solution)/shard_map/ppermute | solution.py:38
  12.9 6.4 %collective-permute-start.37 = (bf16[256,128]{1,0:T(8,128)(2,1)S(1)}, bf16[256,128]{1,0:T(8,128)(2,1)S(1)}, u32[]{:S(2)}, u32[]{:S(2)}) collective-permute-start(bf16[256,128]{1,0:T(8,128)(2,1)S(1)} %begin.3.refs_0_), channel_id=1, source_target_pairs={{0,4},{4,0},{8,12},{12,8},{1,5},{5,1},{9,13},{13,9},{2,6},{6,2},{1... | collective-permute-start | bytes 196616 | tf_op jit(solution)/shard_map/ppermute | solution.py:38
  22.2 7.9 %collective-permute-start.40 = (bf16[256,128]{1,0:T(8,128)(2,1)S(1)}, bf16[256,128]{1,0:T(8,128)(2,1)S(1)}, u32[]{:S(2)}, u32[]{:S(2)}) collective-permute-start(bf16[256,128]{1,0:T(8,128)(2,1)S(1)} %get-tuple-element.92), channel_id=1, source_target_pairs={{0,1},{1,0},{2,3},{3,2},{4,5},{5,4},{6,7},{7,6},{8,9},{9,8},{10,11... | collective-permute-start | bytes 196616 | tf_op jit(solution)/shard_map/ppermute | solution.py:38
  23.7 6.8 %collective-permute-start.41 = (bf16[256,128]{1,0:T(8,128)(2,1)S(1)}, bf16[256,128]{1,0:T(8,128)(2,1)S(1)}, u32[]{:S(2)}, u32[]{:S(2)}) collective-permute-start(bf16[256,128]{1,0:T(8,128)(2,1)S(1)} %get-tuple-element.93), channel_id=1, source_target_pairs={{0,2},{1,3},{2,0},{3,1},{4,6},{5,7},{6,4},{7,5},{8,10},{9,11},{10,... | collective-permute-start | bytes 196616 | tf_op jit(solution)/shard_map/ppermute | solution.py:38
  27.0 6.3 %collective-permute-start.3 = (bf16[256,128]{1,0:T(8,128)(2,1)S(1)}, bf16[256,128]{1,0:T(8,128)(2,1)S(1)}, u32[]{:S(2)}, u32[]{:S(2)}) collective-permute-start(bf16[256,128]{1,0:T(8,128)(2,1)S(1)} %get-tuple-element.63), channel_id=1, source_target_pairs={{0,1},{1,0},{2,3},{3,2},{4,5},{5,4},{6,7},{7,6},{8,9},{9,8},{10,11... | collective-permute-start | bytes 196616 | tf_op jit(solution)/shard_map/ppermute | solution.py:38
  28.6 6.9 %collective-permute-start.4 = (bf16[256,128]{1,0:T(8,128)(2,1)S(1)}, bf16[256,128]{1,0:T(8,128)(2,1)S(1)}, u32[]{:S(2)}, u32[]{:S(2)}) collective-permute-start(bf16[256,128]{1,0:T(8,128)(2,1)S(1)} %get-tuple-element.64), channel_id=1, source_target_pairs={{0,2},{1,3},{2,0},{3,1},{4,6},{5,7},{6,4},{7,5},{8,10},{9,11},{10,... | collective-permute-start | bytes 196616 | tf_op jit(solution)/shard_map/ppermute | solution.py:38
  31.0 7.2 %collective-permute-start.45 = (bf16[256,128]{1,0:T(8,128)(2,1)S(1)}, bf16[256,128]{1,0:T(8,128)(2,1)S(1)}, u32[]{:S(2)}, u32[]{:S(2)}) collective-permute-start(bf16[256,128]{1,0:T(8,128)(2,1)S(1)} %forward_solve.3.refs_0_), channel_id=1, source_target_pairs={{0,12},{4,8},{8,4},{12,0},{1,13},{5,9},{9,5},{13,1},{2,14},{6,10},... | collective-permute-start | bytes 196616 | tf_op jit(solution)/shard_map/ppermute | solution.py:38
  33.3 7.3 %collective-permute-start.44 = (bf16[256,128]{1,0:T(8,128)(2,1)S(1)}, bf16[256,128]{1,0:T(8,128)(2,1)S(1)}, u32[]{:S(2)}, u32[]{:S(2)}) collective-permute-start(bf16[256,128]{1,0:T(8,128)(2,1)S(1)} %forward_solve.3.refs_0_), channel_id=1, source_target_pairs={{0,8},{4,12},{8,0},{12,4},{1,9},{5,13},{9,1},{13,5},{2,10},{6,14},... | collective-permute-start | bytes 196616 | tf_op jit(solution)/shard_map/ppermute | solution.py:38
  33.3 7.3 %collective-permute-start.43 = (bf16[256,128]{1,0:T(8,128)(2,1)S(1)}, bf16[256,128]{1,0:T(8,128)(2,1)S(1)}, u32[]{:S(2)}, u32[]{:S(2)}) collective-permute-start(bf16[256,128]{1,0:T(8,128)(2,1)S(1)} %forward_solve.3.refs_0_), channel_id=1, source_target_pairs={{0,4},{4,0},{8,12},{12,8},{1,5},{5,1},{9,13},{13,9},{2,6},{6,2},{1... | collective-permute-start | bytes 196616 | tf_op jit(solution)/shard_map/ppermute | solution.py:38
  35.8 9.1 %collective-permute-start.8 = (bf16[256,128]{1,0:T(8,128)(2,1)S(1)}, bf16[256,128]{1,0:T(8,128)(2,1)S(1)}, u32[]{:S(2)}, u32[]{:S(2)}) collective-permute-start(bf16[256,128]{1,0:T(8,128)(2,1)S(1)} %forward_solve.2.refs_0_), channel_id=1, source_target_pairs={{0,12},{4,8},{8,4},{12,0},{1,13},{5,9},{9,5},{13,1},{2,14},{6,10},... | collective-permute-start | bytes 196616 | tf_op jit(solution)/shard_map/ppermute | solution.py:38
  38.2 7.3 %collective-permute-start.7 = (bf16[256,128]{1,0:T(8,128)(2,1)S(1)}, bf16[256,128]{1,0:T(8,128)(2,1)S(1)}, u32[]{:S(2)}, u32[]{:S(2)}) collective-permute-start(bf16[256,128]{1,0:T(8,128)(2,1)S(1)} %forward_solve.2.refs_0_), channel_id=1, source_target_pairs={{0,8},{4,12},{8,0},{12,4},{1,9},{5,13},{9,1},{13,5},{2,10},{6,14},... | collective-permute-start | bytes 196616 | tf_op jit(solution)/shard_map/ppermute | solution.py:38
  38.2 7.3 %collective-permute-start.6 = (bf16[256,128]{1,0:T(8,128)(2,1)S(1)}, bf16[256,128]{1,0:T(8,128)(2,1)S(1)}, u32[]{:S(2)}, u32[]{:S(2)}) collective-permute-start(bf16[256,128]{1,0:T(8,128)(2,1)S(1)} %forward_solve.2.refs_0_), channel_id=1, source_target_pairs={{0,4},{4,0},{8,12},{12,8},{1,5},{5,1},{9,13},{13,9},{2,6},{6,2},{1... | collective-permute-start | bytes 196616 | tf_op jit(solution)/shard_map/ppermute | solution.py:38
  41.9 7.8 %collective-permute-start.46 = (bf16[256,128]{1,0:T(8,128)(2,1)S(1)}, bf16[256,128]{1,0:T(8,128)(2,1)S(1)}, u32[]{:S(2)}, u32[]{:S(2)}) collective-permute-start(bf16[256,128]{1,0:T(8,128)(2,1)S(1)} %get-tuple-element.96), channel_id=1, source_target_pairs={{0,1},{1,0},{2,3},{3,2},{4,5},{5,4},{6,7},{7,6},{8,9},{9,8},{10,11... | collective-permute-start | bytes 196616 | tf_op jit(solution)/shard_map/ppermute | solution.py:38
  43.4 6.9 %collective-permute-start.47 = (bf16[256,128]{1,0:T(8,128)(2,1)S(1)}, bf16[256,128]{1,0:T(8,128)(2,1)S(1)}, u32[]{:S(2)}, u32[]{:S(2)}) collective-permute-start(bf16[256,128]{1,0:T(8,128)(2,1)S(1)} %get-tuple-element.97), channel_id=1, source_target_pairs={{0,2},{1,3},{2,0},{3,1},{4,6},{5,7},{6,4},{7,5},{8,10},{9,11},{10,... | collective-permute-start | bytes 196616 | tf_op jit(solution)/shard_map/ppermute | solution.py:38
  46.7 6.5 %collective-permute-start.9 = (bf16[256,128]{1,0:T(8,128)(2,1)S(1)}, bf16[256,128]{1,0:T(8,128)(2,1)S(1)}, u32[]{:S(2)}, u32[]{:S(2)}) collective-permute-start(bf16[256,128]{1,0:T(8,128)(2,1)S(1)} %get-tuple-element.67), channel_id=1, source_target_pairs={{0,1},{1,0},{2,3},{3,2},{4,5},{5,4},{6,7},{7,6},{8,9},{9,8},{10,11... | collective-permute-start | bytes 196616 | tf_op jit(solution)/shard_map/ppermute | solution.py:38
  48.2 7.0 %collective-permute-start.10 = (bf16[256,128]{1,0:T(8,128)(2,1)S(1)}, bf16[256,128]{1,0:T(8,128)(2,1)S(1)}, u32[]{:S(2)}, u32[]{:S(2)}) collective-permute-start(bf16[256,128]{1,0:T(8,128)(2,1)S(1)} %get-tuple-element.68), channel_id=1, source_target_pairs={{0,2},{1,3},{2,0},{3,1},{4,6},{5,7},{6,4},{7,5},{8,10},{9,11},{10,... | collective-permute-start | bytes 196616 | tf_op jit(solution)/shard_map/ppermute | solution.py:38
  49.7 5.5 %collective-permute-start.11 = (bf16[256,128]{1,0:T(8,128)(2,1)S(1)}, bf16[256,128]{1,0:T(8,128)(2,1)S(1)}, u32[]{:S(2)}, u32[]{:S(2)}) collective-permute-start(bf16[256,128]{1,0:T(8,128)(2,1)S(1)} %get-tuple-element.69), channel_id=1, source_target_pairs={{0,3},{1,2},{2,1},{3,0},{4,7},{5,6},{6,5},{7,4},{8,11},{9,10},{10,... | collective-permute-start | bytes 196616 | tf_op jit(solution)/shard_map/ppermute | solution.py:38
  50.7 7.5 %collective-permute-start.51 = (bf16[256,128]{1,0:T(8,128)(2,1)S(1)}, bf16[256,128]{1,0:T(8,128)(2,1)S(1)}, u32[]{:S(2)}, u32[]{:S(2)}) collective-permute-start(bf16[256,128]{1,0:T(8,128)(2,1)S(1)} %get-tuple-element.100.refs_0_), channel_id=1, source_target_pairs={{0,12},{4,8},{8,4},{12,0},{1,13},{5,9},{9,5},{13,1},{2,14},{6,10},... | collective-permute-start | bytes 196616 | tf_op jit(solution)/shard_map/ppermute | solution.py:38
  53.2 7.0 %collective-permute-start.50 = (bf16[256,128]{1,0:T(8,128)(2,1)S(1)}, bf16[256,128]{1,0:T(8,128)(2,1)S(1)}, u32[]{:S(2)}, u32[]{:S(2)}) collective-permute-start(bf16[256,128]{1,0:T(8,128)(2,1)S(1)} %get-tuple-element.100.refs_0_), channel_id=1, source_target_pairs={{0,8},{4,12},{8,0},{12,4},{1,9},{5,13},{9,1},{13,5},{2,10},{6,14},... | collective-permute-start | bytes 196616 | tf_op jit(solution)/shard_map/ppermute | solution.py:38
  53.2 7.0 %collective-permute-start.49 = (bf16[256,128]{1,0:T(8,128)(2,1)S(1)}, bf16[256,128]{1,0:T(8,128)(2,1)S(1)}, u32[]{:S(2)}, u32[]{:S(2)}) collective-permute-start(bf16[256,128]{1,0:T(8,128)(2,1)S(1)} %get-tuple-element.100.refs_0_), channel_id=1, source_target_pairs={{0,4},{4,0},{8,12},{12,8},{1,5},{5,1},{9,13},{13,9},{2,6},{6,2},{1... | collective-permute-start | bytes 196616 | tf_op jit(solution)/shard_map/ppermute | solution.py:38
  55.6 10.5 %collective-permute-start.14 = (bf16[256,128]{1,0:T(8,128)(2,1)S(1)}, bf16[256,128]{1,0:T(8,128)(2,1)S(1)}, u32[]{:S(2)}, u32[]{:S(2)}) collective-permute-start(bf16[256,128]{1,0:T(8,128)(2,1)S(1)} %get-tuple-element.71.refs_0_), channel_id=1, source_target_pairs={{0,12},{4,8},{8,4},{12,0},{1,13},{5,9},{9,5},{13,1},{2,14},{6,10},... | collective-permute-start | bytes 196616 | tf_op jit(solution)/shard_map/ppermute | solution.py:38
  58.2 8.4 %collective-permute-start.13 = (bf16[256,128]{1,0:T(8,128)(2,1)S(1)}, bf16[256,128]{1,0:T(8,128)(2,1)S(1)}, u32[]{:S(2)}, u32[]{:S(2)}) collective-permute-start(bf16[256,128]{1,0:T(8,128)(2,1)S(1)} %get-tuple-element.71.refs_0_), channel_id=1, source_target_pairs={{0,8},{4,12},{8,0},{12,4},{1,9},{5,13},{9,1},{13,5},{2,10},{6,14},... | collective-permute-start | bytes 196616 | tf_op jit(solution)/shard_map/ppermute | solution.py:38
  58.2 8.4 %collective-permute-start.12 = (bf16[256,128]{1,0:T(8,128)(2,1)S(1)}, bf16[256,128]{1,0:T(8,128)(2,1)S(1)}, u32[]{:S(2)}, u32[]{:S(2)}) collective-permute-start(bf16[256,128]{1,0:T(8,128)(2,1)S(1)} %get-tuple-element.71.refs_0_), channel_id=1, source_target_pairs={{0,4},{4,0},{8,12},{12,8},{1,5},{5,1},{9,13},{13,9},{2,6},{6,2},{1... | collective-permute-start | bytes 196616 | tf_op jit(solution)/shard_map/ppermute | solution.py:38
  63.1 7.9 %collective-permute-start.52 = (bf16[256,128]{1,0:T(8,128)(2,1)S(1)}, bf16[256,128]{1,0:T(8,128)(2,1)S(1)}, u32[]{:S(2)}, u32[]{:S(2)}) collective-permute-start(bf16[256,128]{1,0:T(8,128)(2,1)S(1)} %get-tuple-element.102), channel_id=1, source_target_pairs={{0,1},{1,0},{2,3},{3,2},{4,5},{5,4},{6,7},{7,6},{8,9},{9,8},{10,11... | collective-permute-start | bytes 196616 | tf_op jit(solution)/shard_map/ppermute | solution.py:38
  64.6 6.9 %collective-permute-start.53 = (bf16[256,128]{1,0:T(8,128)(2,1)S(1)}, bf16[256,128]{1,0:T(8,128)(2,1)S(1)}, u32[]{:S(2)}, u32[]{:S(2)}) collective-permute-start(bf16[256,128]{1,0:T(8,128)(2,1)S(1)} %get-tuple-element.103), channel_id=1, source_target_pairs={{0,2},{1,3},{2,0},{3,1},{4,6},{5,7},{6,4},{7,5},{8,10},{9,11},{10,... | collective-permute-start | bytes 196616 | tf_op jit(solution)/shard_map/ppermute | solution.py:38
  77.1 6.5 %collective-permute-start.58 = (bf16[128,256]{1,0:T(8,128)(2,1)S(1)}, bf16[128,256]{1,0:T(8,128)(2,1)S(1)}, u32[]{:S(2)}, u32[]{:S(2)}) collective-permute-start(bf16[128,256]{1,0:T(8,128)(2,1)S(1)} %get-tuple-element.105.refs_0_), channel_id=1, source_target_pairs={{0,3},{1,2},{2,1},{3,0},{4,7},{5,6},{6,5},{7,4},{8,11},{9,10},{10,... | collective-permute-start | bytes 196616 | tf_op jit(solution)/shard_map/ppermute | solution.py:38
  77.7 7.4 %collective-permute-start.57 = (bf16[128,256]{1,0:T(8,128)(2,1)S(1)}, bf16[128,256]{1,0:T(8,128)(2,1)S(1)}, u32[]{:S(2)}, u32[]{:S(2)}) collective-permute-start(bf16[128,256]{1,0:T(8,128)(2,1)S(1)} %get-tuple-element.105.refs_0_), channel_id=1, source_target_pairs={{0,2},{1,3},{2,0},{3,1},{4,6},{5,7},{6,4},{7,5},{8,10},{9,11},{10,... | collective-permute-start | bytes 196616 | tf_op jit(solution)/shard_map/ppermute | solution.py:38
  79.2 5.9 %collective-permute-start.56 = (bf16[128,256]{1,0:T(8,128)(2,1)S(1)}, bf16[128,256]{1,0:T(8,128)(2,1)S(1)}, u32[]{:S(2)}, u32[]{:S(2)}) collective-permute-start(bf16[128,256]{1,0:T(8,128)(2,1)S(1)} %get-tuple-element.105.refs_0_), channel_id=1, source_target_pairs={{0,1},{1,0},{2,3},{3,2},{4,5},{5,4},{6,7},{7,6},{8,9},{9,8},{10,11... | collective-permute-start | bytes 196616 | tf_op jit(solution)/shard_map/ppermute | solution.py:38
  81.6 7.6 %collective-permute-start.21 = (bf16[128,256]{1,0:T(8,128)(2,1)S(1)}, bf16[128,256]{1,0:T(8,128)(2,1)S(1)}, u32[]{:S(2)}, u32[]{:S(2)}) collective-permute-start(bf16[128,256]{1,0:T(8,128)(2,1)S(1)} %get-tuple-element.76.refs_0_), channel_id=1, source_target_pairs={{0,3},{1,2},{2,1},{3,0},{4,7},{5,6},{6,5},{7,4},{8,11},{9,10},{10,... | collective-permute-start | bytes 196616 | tf_op jit(solution)/shard_map/ppermute | solution.py:38
  82.2 8.4 %collective-permute-start.20 = (bf16[128,256]{1,0:T(8,128)(2,1)S(1)}, bf16[128,256]{1,0:T(8,128)(2,1)S(1)}, u32[]{:S(2)}, u32[]{:S(2)}) collective-permute-start(bf16[128,256]{1,0:T(8,128)(2,1)S(1)} %get-tuple-element.76.refs_0_), channel_id=1, source_target_pairs={{0,2},{1,3},{2,0},{3,1},{4,6},{5,7},{6,4},{7,5},{8,10},{9,11},{10,... | collective-permute-start | bytes 196616 | tf_op jit(solution)/shard_map/ppermute | solution.py:38
  83.7 7.0 %collective-permute-start.19 = (bf16[128,256]{1,0:T(8,128)(2,1)S(1)}, bf16[128,256]{1,0:T(8,128)(2,1)S(1)}, u32[]{:S(2)}, u32[]{:S(2)}) collective-permute-start(bf16[128,256]{1,0:T(8,128)(2,1)S(1)} %get-tuple-element.76.refs_0_), channel_id=1, source_target_pairs={{0,1},{1,0},{2,3},{3,2},{4,5},{5,4},{6,7},{7,6},{8,9},{9,8},{10,11... | collective-permute-start | bytes 196616 | tf_op jit(solution)/shard_map/ppermute | solution.py:38
  86.2 8.7 %collective-permute-start.59 = (bf16[128,256]{1,0:T(8,128)(2,1)S(1)}, bf16[128,256]{1,0:T(8,128)(2,1)S(1)}, u32[]{:S(2)}, u32[]{:S(2)}) collective-permute-start(bf16[128,256]{1,0:T(8,128)(2,1)S(1)} %get-tuple-element.107), channel_id=1, source_target_pairs={{0,4},{4,0},{8,12},{12,8},{1,5},{5,1},{9,13},{13,9},{2,6},{6,2},{1... | collective-permute-start | bytes 196616 | tf_op jit(solution)/shard_map/ppermute | solution.py:38
  86.4 9.9 %collective-permute-start.60 = (bf16[128,256]{1,0:T(8,128)(2,1)S(1)}, bf16[128,256]{1,0:T(8,128)(2,1)S(1)}, u32[]{:S(2)}, u32[]{:S(2)}) collective-permute-start(bf16[128,256]{1,0:T(8,128)(2,1)S(1)} %get-tuple-element.108), channel_id=1, source_target_pairs={{0,8},{4,12},{8,0},{12,4},{1,9},{5,13},{9,1},{13,5},{2,10},{6,14},... | collective-permute-start | bytes 196616 | tf_op jit(solution)/shard_map/ppermute | solution.py:38
  89.2 7.1 %collective-permute-start.61 = (bf16[128,256]{1,0:T(8,128)(2,1)S(1)}, bf16[128,256]{1,0:T(8,128)(2,1)S(1)}, u32[]{:S(2)}, u32[]{:S(2)}) collective-permute-start(bf16[128,256]{1,0:T(8,128)(2,1)S(1)} %get-tuple-element.109), channel_id=1, source_target_pairs={{0,12},{4,8},{8,4},{12,0},{1,13},{5,9},{9,5},{13,1},{2,14},{6,10},... | collective-permute-start | bytes 196616 | tf_op jit(solution)/shard_map/ppermute | solution.py:38
  91.8 6.8 %collective-permute-start.22 = (bf16[128,256]{1,0:T(8,128)(2,1)S(1)}, bf16[128,256]{1,0:T(8,128)(2,1)S(1)}, u32[]{:S(2)}, u32[]{:S(2)}) collective-permute-start(bf16[128,256]{1,0:T(8,128)(2,1)S(1)} %get-tuple-element.78), channel_id=1, source_target_pairs={{0,4},{4,0},{8,12},{12,8},{1,5},{5,1},{9,13},{13,9},{2,6},{6,2},{1... | collective-permute-start | bytes 196616 | tf_op jit(solution)/shard_map/ppermute | solution.py:38
  91.9 8.3 %collective-permute-start.23 = (bf16[128,256]{1,0:T(8,128)(2,1)S(1)}, bf16[128,256]{1,0:T(8,128)(2,1)S(1)}, u32[]{:S(2)}, u32[]{:S(2)}) collective-permute-start(bf16[128,256]{1,0:T(8,128)(2,1)S(1)} %get-tuple-element.79), channel_id=1, source_target_pairs={{0,8},{4,12},{8,0},{12,4},{1,9},{5,13},{9,1},{13,5},{2,10},{6,14},... | collective-permute-start | bytes 196616 | tf_op jit(solution)/shard_map/ppermute | solution.py:38
  94.9 6.1 %collective-permute-start.24 = (bf16[128,256]{1,0:T(8,128)(2,1)S(1)}, bf16[128,256]{1,0:T(8,128)(2,1)S(1)}, u32[]{:S(2)}, u32[]{:S(2)}) collective-permute-start(bf16[128,256]{1,0:T(8,128)(2,1)S(1)} %get-tuple-element.80), channel_id=1, source_target_pairs={{0,12},{4,8},{8,4},{12,0},{1,13},{5,9},{9,5},{13,1},{2,14},{6,10},... | collective-permute-start | bytes 196616 | tf_op jit(solution)/shard_map/ppermute | solution.py:38
  96.6 6.7 %collective-permute-start.64 = (bf16[128,256]{1,0:T(8,128)(2,1)S(1)}, bf16[128,256]{1,0:T(8,128)(2,1)S(1)}, u32[]{:S(2)}, u32[]{:S(2)}) collective-permute-start(bf16[128,256]{1,0:T(8,128)(2,1)S(1)} %get-tuple-element.111.refs_0_), channel_id=1, source_target_pairs={{0,3},{1,2},{2,1},{3,0},{4,7},{5,6},{6,5},{7,4},{8,11},{9,10},{10,... | collective-permute-start | bytes 196616 | tf_op jit(solution)/shard_map/ppermute | solution.py:38
  97.2 7.6 %collective-permute-start.63 = (bf16[128,256]{1,0:T(8,128)(2,1)S(1)}, bf16[128,256]{1,0:T(8,128)(2,1)S(1)}, u32[]{:S(2)}, u32[]{:S(2)}) collective-permute-start(bf16[128,256]{1,0:T(8,128)(2,1)S(1)} %get-tuple-element.111.refs_0_), channel_id=1, source_target_pairs={{0,2},{1,3},{2,0},{3,1},{4,6},{5,7},{6,4},{7,5},{8,10},{9,11},{10,... | collective-permute-start | bytes 196616 | tf_op jit(solution)/shard_map/ppermute | solution.py:38
  98.7 6.1 %collective-permute-start.62 = (bf16[128,256]{1,0:T(8,128)(2,1)S(1)}, bf16[128,256]{1,0:T(8,128)(2,1)S(1)}, u32[]{:S(2)}, u32[]{:S(2)}) collective-permute-start(bf16[128,256]{1,0:T(8,128)(2,1)S(1)} %get-tuple-element.111.refs_0_), channel_id=1, source_target_pairs={{0,1},{1,0},{2,3},{3,2},{4,5},{5,4},{6,7},{7,6},{8,9},{9,8},{10,11... | collective-permute-start | bytes 196616 | tf_op jit(solution)/shard_map/ppermute | solution.py:38
  101.3 6.9 %collective-permute-start.27 = (bf16[128,256]{1,0:T(8,128)(2,1)S(1)}, bf16[128,256]{1,0:T(8,128)(2,1)S(1)}, u32[]{:S(2)}, u32[]{:S(2)}) collective-permute-start(bf16[128,256]{1,0:T(8,128)(2,1)S(1)} %get-tuple-element.82.refs_0_), channel_id=1, source_target_pairs={{0,3},{1,2},{2,1},{3,0},{4,7},{5,6},{6,5},{7,4},{8,11},{9,10},{10,... | collective-permute-start | bytes 196616 | tf_op jit(solution)/shard_map/ppermute | solution.py:38
  101.8 8.5 %collective-permute-start.26 = (bf16[128,256]{1,0:T(8,128)(2,1)S(1)}, bf16[128,256]{1,0:T(8,128)(2,1)S(1)}, u32[]{:S(2)}, u32[]{:S(2)}) collective-permute-start(bf16[128,256]{1,0:T(8,128)(2,1)S(1)} %get-tuple-element.82.refs_0_), channel_id=1, source_target_pairs={{0,2},{1,3},{2,0},{3,1},{4,6},{5,7},{6,4},{7,5},{8,10},{9,11},{10,... | collective-permute-start | bytes 196616 | tf_op jit(solution)/shard_map/ppermute | solution.py:38
  103.3 7.0 %collective-permute-start.25 = (bf16[128,256]{1,0:T(8,128)(2,1)S(1)}, bf16[128,256]{1,0:T(8,128)(2,1)S(1)}, u32[]{:S(2)}, u32[]{:S(2)}) collective-permute-start(bf16[128,256]{1,0:T(8,128)(2,1)S(1)} %get-tuple-element.82.refs_0_), channel_id=1, source_target_pairs={{0,1},{1,0},{2,3},{3,2},{4,5},{5,4},{6,7},{7,6},{8,9},{9,8},{10,11... | collective-permute-start | bytes 196616 | tf_op jit(solution)/shard_map/ppermute | solution.py:38
  105.8 7.8 %collective-permute-start.65 = (bf16[128,256]{1,0:T(8,128)(2,1)S(1)}, bf16[128,256]{1,0:T(8,128)(2,1)S(1)}, u32[]{:S(2)}, u32[]{:S(2)}) collective-permute-start(bf16[128,256]{1,0:T(8,128)(2,1)S(1)} %get-tuple-element.113), channel_id=1, source_target_pairs={{0,4},{4,0},{8,12},{12,8},{1,5},{5,1},{9,13},{13,9},{2,6},{6,2},{1... | collective-permute-start | bytes 196616 | tf_op jit(solution)/shard_map/ppermute | solution.py:38
  105.9 9.8 %collective-permute-start.66 = (bf16[128,256]{1,0:T(8,128)(2,1)S(1)}, bf16[128,256]{1,0:T(8,128)(2,1)S(1)}, u32[]{:S(2)}, u32[]{:S(2)}) collective-permute-start(bf16[128,256]{1,0:T(8,128)(2,1)S(1)} %get-tuple-element.114), channel_id=1, source_target_pairs={{0,8},{4,12},{8,0},{12,4},{1,9},{5,13},{9,1},{13,5},{2,10},{6,14},... | collective-permute-start | bytes 196616 | tf_op jit(solution)/shard_map/ppermute | solution.py:38
  108.1 7.6 %collective-permute-start.67 = (bf16[128,256]{1,0:T(8,128)(2,1)S(1)}, bf16[128,256]{1,0:T(8,128)(2,1)S(1)}, u32[]{:S(2)}, u32[]{:S(2)}) collective-permute-start(bf16[128,256]{1,0:T(8,128)(2,1)S(1)} %get-tuple-element.115), channel_id=1, source_target_pairs={{0,12},{4,8},{8,4},{12,0},{1,13},{5,9},{9,5},{13,1},{2,14},{6,10},... | collective-permute-start | bytes 196616 | tf_op jit(solution)/shard_map/ppermute | solution.py:38
  111.3 6.8 %collective-permute-start.28 = (bf16[128,256]{1,0:T(8,128)(2,1)S(1)}, bf16[128,256]{1,0:T(8,128)(2,1)S(1)}, u32[]{:S(2)}, u32[]{:S(2)}) collective-permute-start(bf16[128,256]{1,0:T(8,128)(2,1)S(1)} %get-tuple-element.84), channel_id=1, source_target_pairs={{0,4},{4,0},{8,12},{12,8},{1,5},{5,1},{9,13},{13,9},{2,6},{6,2},{1... | collective-permute-start | bytes 196616 | tf_op jit(solution)/shard_map/ppermute | solution.py:38
  111.4 8.3 %collective-permute-start.29 = (bf16[128,256]{1,0:T(8,128)(2,1)S(1)}, bf16[128,256]{1,0:T(8,128)(2,1)S(1)}, u32[]{:S(2)}, u32[]{:S(2)}) collective-permute-start(bf16[128,256]{1,0:T(8,128)(2,1)S(1)} %get-tuple-element.85), channel_id=1, source_target_pairs={{0,8},{4,12},{8,0},{12,4},{1,9},{5,13},{9,1},{13,5},{2,10},{6,14},... | collective-permute-start | bytes 196616 | tf_op jit(solution)/shard_map/ppermute | solution.py:38
  113.6 6.1 %collective-permute-start.30 = (bf16[128,256]{1,0:T(8,128)(2,1)S(1)}, bf16[128,256]{1,0:T(8,128)(2,1)S(1)}, u32[]{:S(2)}, u32[]{:S(2)}) collective-permute-start(bf16[128,256]{1,0:T(8,128)(2,1)S(1)} %get-tuple-element.86), channel_id=1, source_target_pairs={{0,12},{4,8},{8,4},{12,0},{1,13},{5,9},{9,5},{13,1},{2,14},{6,10},... | collective-permute-start | bytes 196616 | tf_op jit(solution)/shard_map/ppermute | solution.py:38
  116.1 5.9 %collective-permute-start.70 = (bf16[128,256]{1,0:T(8,128)(2,1)S(1)}, bf16[128,256]{1,0:T(8,128)(2,1)S(1)}, u32[]{:S(2)}, u32[]{:S(2)}) collective-permute-start(bf16[128,256]{1,0:T(8,128)(2,1)S(1)} %backward_solve.3.refs_0_), channel_id=1, source_target_pairs={{0,3},{1,2},{2,1},{3,0},{4,7},{5,6},{6,5},{7,4},{8,11},{9,10},{10,... | collective-permute-start | bytes 196616 | tf_op jit(solution)/shard_map/ppermute | solution.py:38
  116.7 6.9 %collective-permute-start.69 = (bf16[128,256]{1,0:T(8,128)(2,1)S(1)}, bf16[128,256]{1,0:T(8,128)(2,1)S(1)}, u32[]{:S(2)}, u32[]{:S(2)}) collective-permute-start(bf16[128,256]{1,0:T(8,128)(2,1)S(1)} %backward_solve.3.refs_0_), channel_id=1, source_target_pairs={{0,2},{1,3},{2,0},{3,1},{4,6},{5,7},{6,4},{7,5},{8,10},{9,11},{10,... | collective-permute-start | bytes 196616 | tf_op jit(solution)/shard_map/ppermute | solution.py:38
  120.0 7.4 %collective-permute-start.33 = (bf16[128,256]{1,0:T(8,128)(2,1)S(1)}, bf16[128,256]{1,0:T(8,128)(2,1)S(1)}, u32[]{:S(2)}, u32[]{:S(2)}) collective-permute-start(bf16[128,256]{1,0:T(8,128)(2,1)S(1)} %backward_solve.2.refs_0_), channel_id=1, source_target_pairs={{0,3},{1,2},{2,1},{3,0},{4,7},{5,6},{6,5},{7,4},{8,11},{9,10},{10,... | collective-permute-start | bytes 196616 | tf_op jit(solution)/shard_map/ppermute | solution.py:38
  120.5 8.5 %collective-permute-start.32 = (bf16[128,256]{1,0:T(8,128)(2,1)S(1)}, bf16[128,256]{1,0:T(8,128)(2,1)S(1)}, u32[]{:S(2)}, u32[]{:S(2)}) collective-permute-start(bf16[128,256]{1,0:T(8,128)(2,1)S(1)} %backward_solve.2.refs_0_), channel_id=1, source_target_pairs={{0,2},{1,3},{2,0},{3,1},{4,6},{5,7},{6,4},{7,5},{8,10},{9,11},{10,... | collective-permute-start | bytes 196616 | tf_op jit(solution)/shard_map/ppermute | solution.py:38
  122.0 7.0 %collective-permute-start.31 = (bf16[128,256]{1,0:T(8,128)(2,1)S(1)}, bf16[128,256]{1,0:T(8,128)(2,1)S(1)}, u32[]{:S(2)}, u32[]{:S(2)}) collective-permute-start(bf16[128,256]{1,0:T(8,128)(2,1)S(1)} %backward_solve.2.refs_0_), channel_id=1, source_target_pairs={{0,1},{1,0},{2,3},{3,2},{4,5},{5,4},{6,7},{7,6},{8,9},{9,8},{10,11... | collective-permute-start | bytes 196616 | tf_op jit(solution)/shard_map/ppermute | solution.py:38
  124.6 8.3 %collective-permute-start.71 = (bf16[128,256]{1,0:T(8,128)(2,1)S(1)}, bf16[128,256]{1,0:T(8,128)(2,1)S(1)}, u32[]{:S(2)}, u32[]{:S(2)}) collective-permute-start(bf16[128,256]{1,0:T(8,128)(2,1)S(1)} %get-tuple-element.117), channel_id=1, source_target_pairs={{0,4},{4,0},{8,12},{12,8},{1,5},{5,1},{9,13},{13,9},{2,6},{6,2},{1... | collective-permute-start | bytes 196616 | tf_op jit(solution)/shard_map/ppermute | solution.py:38
  124.7 10.6 %collective-permute-start.72 = (bf16[128,256]{1,0:T(8,128)(2,1)S(1)}, bf16[128,256]{1,0:T(8,128)(2,1)S(1)}, u32[]{:S(2)}, u32[]{:S(2)}) collective-permute-start(bf16[128,256]{1,0:T(8,128)(2,1)S(1)} %get-tuple-element.118), channel_id=1, source_target_pairs={{0,8},{4,12},{8,0},{12,4},{1,9},{5,13},{9,1},{13,5},{2,10},{6,14},... | collective-permute-start | bytes 196616 | tf_op jit(solution)/shard_map/ppermute | solution.py:38
  127.4 7.9 %collective-permute-start.73 = (bf16[128,256]{1,0:T(8,128)(2,1)S(1)}, bf16[128,256]{1,0:T(8,128)(2,1)S(1)}, u32[]{:S(2)}, u32[]{:S(2)}) collective-permute-start(bf16[128,256]{1,0:T(8,128)(2,1)S(1)} %get-tuple-element.119), channel_id=1, source_target_pairs={{0,12},{4,8},{8,4},{12,0},{1,13},{5,9},{9,5},{13,1},{2,14},{6,10},... | collective-permute-start | bytes 196616 | tf_op jit(solution)/shard_map/ppermute | solution.py:38
  130.1 5.6 %collective-permute-start.34 = (bf16[128,256]{1,0:T(8,128)(2,1)S(1)}, bf16[128,256]{1,0:T(8,128)(2,1)S(1)}, u32[]{:S(2)}, u32[]{:S(2)}) collective-permute-start(bf16[128,256]{1,0:T(8,128)(2,1)S(1)} %get-tuple-element.88), channel_id=1, source_target_pairs={{0,4},{4,0},{8,12},{12,8},{1,5},{5,1},{9,13},{13,9},{2,6},{6,2},{1... | collective-permute-start | bytes 196616 | tf_op jit(solution)/shard_map/ppermute | solution.py:38
  130.1 5.5 %collective-permute-start.35 = (bf16[128,256]{1,0:T(8,128)(2,1)S(1)}, bf16[128,256]{1,0:T(8,128)(2,1)S(1)}, u32[]{:S(2)}, u32[]{:S(2)}) collective-permute-start(bf16[128,256]{1,0:T(8,128)(2,1)S(1)} %get-tuple-element.89), channel_id=1, source_target_pairs={{0,8},{4,12},{8,0},{12,4},{1,9},{5,13},{9,1},{13,5},{2,10},{6,14},... | collective-permute-start | bytes 196616 | tf_op jit(solution)/shard_map/ppermute | solution.py:38
  132.9 6.1 %collective-permute-start.36 = (bf16[128,256]{1,0:T(8,128)(2,1)S(1)}, bf16[128,256]{1,0:T(8,128)(2,1)S(1)}, u32[]{:S(2)}, u32[]{:S(2)}) collective-permute-start(bf16[128,256]{1,0:T(8,128)(2,1)S(1)} %get-tuple-element.90), channel_id=1, source_target_pairs={{0,12},{4,8},{8,4},{12,0},{1,13},{5,9},{9,5},{13,1},{2,14},{6,10},... | collective-permute-start | bytes 196616 | tf_op jit(solution)/shard_map/ppermute | solution.py:38
  (22 other events, 142.6 us)

commit v2 on v1

v2 whole, which is shorter than its diff:
```python
import jax
import jax.numpy as jnp
from jax import lax
from jax.experimental import pallas as pl
from jax.experimental.pallas import tpu as pltpu
from jax.sharding import PartitionSpec as P


LEVELS = 3
RELAYED = ("back1",)
HIGH_PREC = lax.Precision.HIGHEST
F32 = jnp.float32
BF16 = jnp.bfloat16

SMEM = pl.BlockSpec(memory_space=pltpu.SMEM)
VMEM = pl.BlockSpec(memory_space=pltpu.VMEM)
HBM = pl.BlockSpec(memory_space=pltpu.HBM)


def partner(index, step, count):
    if count & (count - 1) == 0:
        return index ^ step
    return (index + step) % count


def source(index, step, count):
    if count & (count - 1) == 0:
        return index ^ step
    return (index + count - step) % count


def send(value, axis, step, count):
    pairs = [(index, partner(index, step, count)) for index in range(count)]
    return lax.ppermute(value, axis, pairs)


def scatter_order(count):
    return range(1, count)


def gather_order(count):
    return reversed(range(1, count))


SMALL, LARGE = 16 * 1024 * 1024, 16 * 1024 * 1024


def call(body, outs, specs, operands, flops, scratch=()):
    size = sum(x.size * x.dtype.itemsize for x in operands)
    return pl.pallas_call(
        body,
        out_shape=[jax.ShapeDtypeStruct(shape, dtype) for shape, dtype in outs],
        in_specs=specs,
        out_specs=[VMEM] * len(outs),
        scratch_shapes=list(scratch),
        cost_estimate=pl.CostEstimate(flops=flops, bytes_accessed=size, transcendentals=0),
        compiler_params=pltpu.CompilerParams(vmem_limit_bytes=LARGE if HBM in specs else SMALL),
    )(*operands)


def gather(value, axis, count, name=""):
    received = [value] + [None] * (count - 1)
    if count == 4 and name in RELAYED:
        received[2] = send(value, axis, 2, count)
        received[1] = send(value, axis, 1, count)
        received[3] = send(received[2], axis, 1, count)
        return received
    for step in gather_order(count):
        received[step] = send(value, axis, step, count)
    return received


def add_pair(first, second):
    def body(first_ref, second_ref, out_ref):
        out_ref[...] = (first_ref[...].astype(F32) + second_ref[...].astype(F32)).astype(BF16)

    return call(body, [(first.shape, BF16)], [VMEM] * 2, [first, second], first.size)[0]


def scatter(values, axis, count, name=""):
    received = [values[0]] + [None] * (count - 1)
    if count == 4 and name in RELAYED:
        passed = send(values[3], axis, 1, count)
        received[1] = send(values[1], axis, 1, count)
        received[2] = send(add_pair(values[2], passed), axis, 2, count)
        return received[:3]
    for step in scatter_order(count):
        received[step] = send(values[step], axis, step, count)
    return received


def solve_dot(a, b):
    return jnp.dot(a, b, precision=HIGH_PREC, preferred_element_type=F32)


def total_of(refs):
    total = refs[0][...].astype(F32)
    for ref in refs[1:]:
        total = total + ref[...].astype(F32)
    return total


def products(blocks, weights, fields, axes, stacked=False, fetch=None):
    rows, cols = lax.axis_size("prow"), lax.axis_size("pcol")
    forward = axes == ("prow", "pcol")
    back_count, out_count = (rows, cols) if forward else (cols, rows)
    shape = fields[0].shape

    def body(weight_ref, blocks_ref, *refs):
        if fetch is not None:
            copy = pltpu.make_async_copy(refs[back_count], refs[-2], refs[-1])
            copy.start()
        ins = refs[:back_count]
        outs = refs[back_count + (fetch is not None) :]
        here_in, here_out = lax.axis_index(axes[0]), lax.axis_index(axes[1])
        for step in reversed(range(out_count)):
            target = partner(here_out, step, out_count)
            total = None
            for back in range(back_count):
                origin = source(here_in, back, back_count)
                block = target * rows + origin if forward else origin * rows + target
                if forward:
                    term = jnp.dot(blocks_ref[block], ins[back][...], preferred_element_type=F32)
                else:
                    term = jnp.dot(ins[back][...], blocks_ref[block], preferred_element_type=F32)
                term = term * weight_ref[block]
                total = term if total is None else total + term
            if stacked:
                outs[0][step] = total.astype(BF16)
            else:
                outs[step][...] = total.astype(BF16)
        if fetch is not None:
            copy.wait()

    if stacked:
        outs = [((out_count,) + shape, BF16)]
    else:
        outs = [(shape, BF16)] * out_count
    specs = [SMEM, VMEM] + [VMEM] * back_count
    operands = [weights, blocks] + list(fields)
    scratch = []
    if fetch is not None:
        specs.append(HBM)
        operands.append(fetch)
        outs.append((fetch.shape, fetch.dtype))
        scratch.append(pltpu.SemaphoreType.DMA)
    return call(
        body, outs, specs, operands, 2 * rows * cols * shape[0] * shape[1] * max(shape), scratch
    )


def load(blocks, after):
    def body(blocks_ref, after_ref, out_ref, sem):
        copy = pltpu.make_async_copy(blocks_ref, out_ref, sem)
        copy.start()
        copy.wait()

    return call(
        body,
        [(blocks.shape, blocks.dtype)],
        [HBM, VMEM],
        [blocks, after],
        0,
        [pltpu.SemaphoreType.DMA],
    )[0]


def weigh(scales, pattern, count):
    return (scales * pattern.astype(F32)).reshape(count)


def shards(
    factor,
    factor_scale,
    sub_pattern,
    coupling,
    coupling_scale,
    top_pattern,
    diag_inverse,
    top_inverse,
    rhs_sub,
    rhs_top,
):
    size = factor.shape[5]
    cols = factor.shape[2]
    rows = factor.shape[3]
    layers = lax.axis_size("layer")
    width = rhs_sub.shape[-1]
    chunk = width // layers
    blocks = factor.reshape(rows * cols, size, size)
    links = coupling.reshape(rows * cols, size, size)
    weights = weigh(factor_scale, sub_pattern, rows * cols)
    link_weights = weigh(coupling_scale, top_pattern, rows * cols)
    inverse = diag_inverse.reshape(size, size)
    top_matrix = top_inverse.reshape(size, size)
    own_rhs = rhs_sub.reshape(size, width)
    top_rhs = rhs_top.reshape(size, width)
    solve_flops = 12 * size * size * chunk
    tall, flat = (size, chunk), (chunk, size)

    def window(index):
        return slice(index * chunk, (index + 1) * chunk)

    def moving_window(index):
        return pl.ds(pl.multiple_of(index * chunk, chunk), chunk)

    def begin_loading():
        def body(inv_hbm, rhs_hbm, field_ref, inv_ref, rhs_ref, sems):
            copies = [
                pltpu.make_async_copy(inv_hbm, inv_ref, sems.at[0]),
                pltpu.make_async_copy(rhs_hbm, rhs_ref, sems.at[1]),
            ]
            for copy in copies:
                copy.start()
            for copy in copies:
                copy.wait()
            field_ref[...] = solve_dot(inv_ref[...], rhs_ref[:, window(0)]).astype(BF16)

        return call(
            body,
            [(tall, BF16), (inverse.shape, F32), (own_rhs.shape, F32)],
            [HBM] * 2,
            [inverse, own_rhs],
            solve_flops,
            [pltpu.SemaphoreType.DMA((2,))],
        )

    def begin(index):
        def body(inv_ref, rhs_ref, out_ref):
            out_ref[...] = solve_dot(inv_ref[...], rhs_ref[:, window(index)]).astype(BF16)

        return call(body, [(tall, BF16)], [VMEM] * 2, [inverse, own_rhs], solve_flops)[0]

    def forward_solve(index, parts, last):
        def body(inv_ref, rhs_ref, *refs):
            lower = total_of(refs[: len(parts)])
            outs = refs[len(parts) :]
            solved = solve_dot(inv_ref[...], rhs_ref[:, window(index)] - lower)
            outs[0][...] = solved.astype(BF16)
            if last:
                outs[1][...] = solved.T

        return call(
            body,
            [(tall, BF16)] + [(flat, F32)] * last,
            [VMEM] * (2 + len(parts)),
            [inverse, own_rhs] + list(parts),
            solve_flops,
        )

    def pick_other(stacks):
        def body(*refs):
            here = lax.axis_index("layer")
            for step in range(1, layers):
                for index in range(layers):

                    @pl.when(partner(here, step, layers) == index)
                    def _(step=step, index=index):
                        refs[layers + step - 1][...] = refs[index][...]

        return call(
            body,
            [(stacks[0].shape, BF16)] * (layers - 1),
            [VMEM] * layers,
            list(stacks),
            stacks[0].size,
        )

    def merge(stacks, others):
        def body(*refs):
            here = lax.axis_index("layer")
            outs = refs[2 * layers - 1 :]
            for index in range(layers):

                @pl.when(here == index)
                def _(index=index):
                    for step in range(cols):
                        total = refs[index][step].astype(F32)
                        for other in refs[layers : 2 * layers - 1]:
                            total = total + other[step].astype(F32)
                        outs[step][...] = total.astype(BF16)

        return call(
            body,
            [(tall, BF16)] * cols,
            [VMEM] * (2 * layers - 1),
            list(stacks) + list(others),
            stacks[0].size,
        )

    def top_solve(parts):
        def body(top_ref, rhs_ref, *refs):
            here = lax.axis_index("layer")
            merged = total_of(refs[: len(parts)])
            outs = refs[len(parts) :]
            half = solve_dot(top_ref[...], rhs_ref[:, moving_window(here)] - merged)
            answer = solve_dot(half.T, top_ref[...])
            outs[0][...] = answer
            outs[1][...] = answer.astype(BF16)

        return call(
            body,
            [(flat, F32), (flat, BF16)],
            [VMEM] * (2 + len(parts)),
            [top_matrix, top_rhs] + list(parts),
            2 * solve_flops,
        )

    def backward_first(slot, solved, parts):
        def body(inv_ref, *refs):
            here = lax.axis_index("layer")
            known_ref, out_ref = refs[-2:]
            coupled = total_of(refs[layers:-2])
            chosen = refs[0][...]
            for index in range(1, layers):
                chosen = jnp.where(partner(here, slot, layers) == index, refs[index][...], chosen)
            known = chosen - coupled
            known_ref[...] = known
            out_ref[...] = solve_dot(known, inv_ref[...]).astype(BF16)

        return call(
            body,
            [(flat, F32), (flat, BF16)],
            [VMEM] * (1 + layers + len(parts)),
            [inverse] + list(solved) + list(parts),
            solve_flops,
        )

    def backward_solve(known, parts):
        def body(inv_ref, known_ref, *refs):
            upper = total_of(refs[:-1])
            refs[-1][...] = solve_dot(known_ref[...] - upper, inv_ref[...]).astype(BF16)

        return call(
            body,
            [(flat, BF16)],
            [VMEM] * (2 + len(parts)),
            [inverse, known] + list(parts),
            solve_flops,
        )[0]

    def finish(known, parts, tops):
        terms = len(parts[0])

        def body(inv_ref, *refs):
            here = lax.axis_index("layer")
            out_ref, top_ref = refs[-2:]
            for slot in range(layers):
                window_ref = moving_window(partner(here, slot, layers))
                top_ref[:, window_ref] = refs[slot][...].T
                known_ref = refs[layers + slot]
                low = 2 * layers + slot * terms
                upper = total_of(refs[low : low + terms])
                answer = solve_dot(known_ref[...] - upper, inv_ref[...])
                out_ref[:, window_ref] = answer.T

        operands = [inverse] + list(tops) + list(known) + [x for group in parts for x in group]
        return call(
            body, [((size, width), F32)] * 2, [VMEM] * len(operands), operands, layers * solve_flops
        )

    group = range(layers)
    down, up = ("prow", "pcol"), ("pcol", "prow")
    first, inverse, own_rhs = begin_loading()
    field = [first] + [begin(i) for i in group if i]
    blocks = load(blocks, field[-1])
    solved = [None] * layers
    for sweep in range(LEVELS - 1):
        last = sweep == LEVELS - 2
        for i in group:
            gathered = gather(field[i], "prow", rows, f"forward{sweep}")
            if last and i == 0:
                *sums, links = products(blocks, weights, gathered, down, fetch=links)
            else:
                sums = products(blocks, weights, gathered, down)
            results = forward_solve(i, scatter(sums, "pcol", cols), last)
            field[i] = results[0]
            if last:
                solved[i] = results[1]
    stacks = []
    for i in group:
        stacks += products(
            links, link_weights, gather(field[i], "prow", rows, "links"), down, stacked=True
        )
    others = [
        send(value, "layer", step + 1, layers) for step, value in enumerate(pick_other(stacks))
    ]
    received = [None] * cols
    shares = merge(stacks, others)
    for step in reversed(range(cols)):
        received[step] = send(shares[step], "pcol", step, cols) if step else shares[0]
    top_own, top_field = top_solve(received)
    tops = [top_own] + [send(top_own, "layer", step, layers) for step in range(1, layers)]
    gathered = [None] * cols
    for step in reversed(range(cols)):
        gathered[step] = send(top_field, "pcol", step, cols) if step else top_field
    known, field = [None] * layers, [None] * layers
    for slot in group:
        values = gathered
        if slot:
            values = [send(value, "layer", slot, layers) for value in gathered]
        sums = products(links, link_weights, values, up)
        coupled = scatter(sums, "prow", rows, "couple")
        known[slot], field[slot] = backward_first(slot, solved, coupled)
    for sweep in range(LEVELS - 1):
        parts = [None] * layers
        for slot in group:
            sums = products(blocks, weights, gather(field[slot], "pcol", cols), up)
            parts[slot] = scatter(sums, "prow", rows, f"back{sweep}")
            if sweep < LEVELS - 2:
                field[slot] = backward_solve(known[slot], parts[slot])
    answer, top = finish(known, parts, tops)
    return answer.reshape(rhs_sub.shape), top.reshape(rhs_top.shape)


def solution(mesh):
    blocked = P("layer", "prow", None, None, "pcol", None, None)
    scales = P("layer", "prow", None, None, "pcol")
    lower = P("layer", "prow", "pcol", None, None)
    upper = P("prow", "pcol", None, None)
    return jax.shard_map(
        shards,
        mesh=mesh,
        in_specs=(blocked, scales, scales, blocked, scales, scales, lower, upper, lower, upper),
        out_specs=(lower, upper),
        check_vma=False,
    )
```

time: 140 us -> 136 us (0.971)
  starting transfers between devices: 97.5 us -> 91.6 us
  waiting for transfers between devices: 14.1 us -> 15.6 us
  other arithmetic: 2.19 us -> 0.74 us
    ppermute x74 -> x72, starting transfers between devices: 97.5 us -> 91.6 us  [send(): return lax.ppermute(value, axis, pairs)]
    ppermute x74 -> x72, waiting for transfers between devices: 14.1 us -> 15.6 us  [send(): return lax.ppermute(value, axis, pairs)]
    reshape x2 -> x0, other arithmetic: 1.46 us -> none  [shards(): return (answer.reshape(rhs_sub.shape), top.reshape(rhs_top.shape))]
    unnamed x24 -> x22, local copies, waits for them, and re-layouts: 5.12 us -> 6.41 us
    pallas_call x28 -> x29, Pallas kernels: 19.9 us -> 19.9 us  [call(): pl.pallas_call(body, out_shape=[jax.ShapeDtypeStruct(shape, dtype) for sh...]
  transfers between devices with their start and end apart: 74 -> 72, of which waited for: 7 -> 16; matrix products, arithmetic and copies ran while one was open for 1% -> 1% of each run, Pallas kernels for 14% -> 11%
where the time goes in v2:
time: 136 us; the launch traced here: 135 us
  starting transfers between devices  91.6 us (67%)
  Pallas kernels  19.9 us (15%)
  waiting for transfers between devices  15.6 us (11%)
  local copies, waits for them, and re-layouts  6.58 us (5%)
    ppermute x72, starting transfers between devices, send(): return lax.ppermute(value, axis, pairs)  91.6 us
    pallas_call x29, Pallas kernels, call(): pl.pallas_call(body, out_shape=[jax.ShapeDtypeStruct(shape, dtype) for sh...  19.9 us
    ppermute x72, waiting for transfers between devices, send(): return lax.ppermute(value, axis, pairs)  15.6 us
    unnamed x22, local copies, waits for them, and re-layouts  6.41 us
  transfers between devices with their start and end apart: 72, of which 16 were waited for; matrix products, arithmetic and copies ran while one was open for 1% of the time, Pallas kernels for 11%

profile of v2, /device:TPU:0, one launch (start us, length us, event | category | flops | bytes accessed | tf_op | source)
XLA Modules:
  0.0 135.5 jit_solution(6358429283272265325)
XLA Ops:
  1.6 0.9 copy-done.8
  3.4 5.1 %collective-permute-start.17 = (bf16[256,128]{1,0:T(8,128)(2,1)S(1)}, bf16[256,128]{1,0:T(8,128)(2,1)S(1)}, u32[]{:S(2)}, u32[]{:S(2)}) collective-permute-start(bf16[256,128]{1,0:T(8,128)(2,1)S(1)} %shard_map.114.after_ref.refs_0_), channel_id=1, source_target_pairs={{0,12},{4,8},{8,4},{12,0},{1,13},{5,9},{9,5},{13,1},{2,14},{6,10},... | collective-permute-start | bytes 196616 | tf_op jit(solution)/shard_map/ppermute | solution.py:34
  9.2 3.7 %collective-permute-start.2 = (bf16[256,128]{1,0:T(8,128)(2,1)S(1)}, bf16[256,128]{1,0:T(8,128)(2,1)S(1)}, u32[]{:S(2)}, u32[]{:S(2)}) collective-permute-start(bf16[256,128]{1,0:T(8,128)(2,1)S(1)} %get-tuple-element.64.refs_0_), channel_id=1, source_target_pairs={{0,12},{4,8},{8,4},{12,0},{1,13},{5,9},{9,5},{13,1},{2,14},{6,10},... | collective-permute-start | bytes 196616 | tf_op jit(solution)/shard_map/ppermute | solution.py:34
  14.5 1.6 %copy-done.3 = bf16[1,1,4,4,1,256,256]{6,5,4,3,2,1,0:T(8,128)(2,1)S(1)} copy-done((bf16[1,1,4,4,1,256,256]{6,5,4,3,2,1,0:T(8,128)(2,1)S(1)}, bf16[1,1,4,4,1,256,256]{6,5,4,3,2,1,0:T(8,128)(2,1)}, u32[]{:S(2)}) %copy-start.3) | copy-done | bytes 2097176
  17.0 1.2 shard_map.121
  18.3 1.3 collective-permute-start.18
  19.6 1.5 %collective-permute-start.19 = (bf16[256,128]{1,0:T(8,128)(2,1)S(1)}, bf16[256,128]{1,0:T(8,128)(2,1)S(1)}, u32[]{:S(2)}, u32[]{:S(2)}) collective-permute-start(bf16[256,128]{1,0:T(8,128)(2,1)S(1)} %get-tuple-element.77), channel_id=1, source_target_pairs={{0,2},{1,3},{2,0},{3,1},{4,6},{5,7},{6,4},{7,5},{8,10},{9,11},{10,... | collective-permute-start | bytes 196616 | tf_op jit(solution)/shard_map/ppermute | solution.py:34
  21.8 1.2 shard_map.116
  23.1 1.3 collective-permute-start.3
  24.4 1.5 %collective-permute-start.4 = (bf16[256,128]{1,0:T(8,128)(2,1)S(1)}, bf16[256,128]{1,0:T(8,128)(2,1)S(1)}, u32[]{:S(2)}, u32[]{:S(2)}) collective-permute-start(bf16[256,128]{1,0:T(8,128)(2,1)S(1)} %get-tuple-element.67), channel_id=1, source_target_pairs={{0,2},{1,3},{2,0},{3,1},{4,6},{5,7},{6,4},{7,5},{8,10},{9,11},{10,... | collective-permute-start | bytes 196616 | tf_op jit(solution)/shard_map/ppermute | solution.py:34
  27.1 2.9 %collective-permute-start.23 = (bf16[256,128]{1,0:T(8,128)(2,1)S(1)}, bf16[256,128]{1,0:T(8,128)(2,1)S(1)}, u32[]{:S(2)}, u32[]{:S(2)}) collective-permute-start(bf16[256,128]{1,0:T(8,128)(2,1)S(1)} %shard_map.122.refs_0_), channel_id=1, source_target_pairs={{0,12},{4,8},{8,4},{12,0},{1,13},{5,9},{9,5},{13,1},{2,14},{6,10},... | collective-permute-start | bytes 196616 | tf_op jit(solution)/shard_map/ppermute | solution.py:34
  30.0 1.6 %collective-permute-start.21 = (bf16[256,128]{1,0:T(8,128)(2,1)S(1)}, bf16[256,128]{1,0:T(8,128)(2,1)S(1)}, u32[]{:S(2)}, u32[]{:S(2)}) collective-permute-start(bf16[256,128]{1,0:T(8,128)(2,1)S(1)} %shard_map.122.refs_0_), channel_id=1, source_target_pairs={{0,4},{4,0},{8,12},{12,8},{1,5},{5,1},{9,13},{13,9},{2,6},{6,2},{1... | collective-permute-start | bytes 196616 | tf_op jit(solution)/shard_map/ppermute | solution.py:34
  31.9 2.9 %collective-permute-start.8 = (bf16[256,128]{1,0:T(8,128)(2,1)S(1)}, bf16[256,128]{1,0:T(8,128)(2,1)S(1)}, u32[]{:S(2)}, u32[]{:S(2)}) collective-permute-start(bf16[256,128]{1,0:T(8,128)(2,1)S(1)} %shard_map.117.refs_0_), channel_id=1, source_target_pairs={{0,12},{4,8},{8,4},{12,0},{1,13},{5,9},{9,5},{13,1},{2,14},{6,10},... | collective-permute-start | bytes 196616 | tf_op jit(solution)/shard_map/ppermute | solution.py:34
  34.8 1.6 %collective-permute-start.6 = (bf16[256,128]{1,0:T(8,128)(2,1)S(1)}, bf16[256,128]{1,0:T(8,128)(2,1)S(1)}, u32[]{:S(2)}, u32[]{:S(2)}) collective-permute-start(bf16[256,128]{1,0:T(8,128)(2,1)S(1)} %shard_map.117.refs_0_), channel_id=1, source_target_pairs={{0,4},{4,0},{8,12},{12,8},{1,5},{5,1},{9,13},{13,9},{2,6},{6,2},{1... | collective-permute-start | bytes 196616 | tf_op jit(solution)/shard_map/ppermute | solution.py:34
  36.5 1.2 shard_map.123
  37.7 1.5 %collective-permute-start.24 = (bf16[256,128]{1,0:T(8,128)(2,1)S(1)}, bf16[256,128]{1,0:T(8,128)(2,1)S(1)}, u32[]{:S(2)}, u32[]{:S(2)}) collective-permute-start(bf16[256,128]{1,0:T(8,128)(2,1)S(1)} %get-tuple-element.80), channel_id=1, source_target_pairs={{0,1},{1,0},{2,3},{3,2},{4,5},{5,4},{6,7},{7,6},{8,9},{9,8},{10,11... | collective-permute-start | bytes 196616 | tf_op jit(solution)/shard_map/ppermute | solution.py:34
  39.3 1.5 %collective-permute-start.25 = (bf16[256,128]{1,0:T(8,128)(2,1)S(1)}, bf16[256,128]{1,0:T(8,128)(2,1)S(1)}, u32[]{:S(2)}, u32[]{:S(2)}) collective-permute-start(bf16[256,128]{1,0:T(8,128)(2,1)S(1)} %get-tuple-element.81), channel_id=1, source_target_pairs={{0,2},{1,3},{2,0},{3,1},{4,6},{5,7},{6,4},{7,5},{8,10},{9,11},{10,... | collective-permute-start | bytes 196616 | tf_op jit(solution)/shard_map/ppermute | solution.py:34
  41.3 1.4 %shard_map.118 = (bf16[256,128]{1,0:T(8,128)(2,1)S(1)}, bf16[256,128]{1,0:T(8,128)(2,1)S(1)}, bf16[256,128]{1,0:T(8,128)(2,1)S(1)}, bf16[256,128]{1,0:T(8,128)(2,1)S(1)}, bf16[16,256,256]{2,1,0:T(8,128)(2,1)S(1)}) custom-call(f32[16]{0:T(128)S(1)} %reshape.39.weight_ref, bf16[16,256,256]{2,1,0:T(8,128)(2,1)S(1)} %shard_map.115.blocks_ref, ...), custom_call_target="tpu_custom_call" | custom-call | flops 268435456 | bytes 4456512 | tf_op jit(solution)/shard_map/pallas_call | solution.py:50
  42.7 1.3 copy-done
  44.0 1.5 %collective-permute-start.9 = (bf16[256,128]{1,0:T(8,128)(2,1)S(1)}, bf16[256,128]{1,0:T(8,128)(2,1)S(1)}, u32[]{:S(2)}, u32[]{:S(2)}) collective-permute-start(bf16[256,128]{1,0:T(8,128)(2,1)S(1)} %get-tuple-element.71), channel_id=1, source_target_pairs={{0,1},{1,0},{2,3},{3,2},{4,5},{5,4},{6,7},{7,6},{8,9},{9,8},{10,11... | collective-permute-start | bytes 196616 | tf_op jit(solution)/shard_map/ppermute | solution.py:34
  45.5 1.5 %collective-permute-start.10 = (bf16[256,128]{1,0:T(8,128)(2,1)S(1)}, bf16[256,128]{1,0:T(8,128)(2,1)S(1)}, u32[]{:S(2)}, u32[]{:S(2)}) collective-permute-start(bf16[256,128]{1,0:T(8,128)(2,1)S(1)} %get-tuple-element.72), channel_id=1, source_target_pairs={{0,2},{1,3},{2,0},{3,1},{4,6},{5,7},{6,4},{7,5},{8,10},{9,11},{10,... | collective-permute-start | bytes 196616 | tf_op jit(solution)/shard_map/ppermute | solution.py:34
  48.0 2.8 %collective-permute-start.29 = (bf16[256,128]{1,0:T(8,128)(2,1)S(1)}, bf16[256,128]{1,0:T(8,128)(2,1)S(1)}, u32[]{:S(2)}, u32[]{:S(2)}) collective-permute-start(bf16[256,128]{1,0:T(8,128)(2,1)S(1)} %get-tuple-element.83.refs_0_), channel_id=1, source_target_pairs={{0,12},{4,8},{8,4},{12,0},{1,13},{5,9},{9,5},{13,1},{2,14},{6,10},... | collective-permute-start | bytes 196616 | tf_op jit(solution)/shard_map/ppermute | solution.py:34
  50.8 1.7 %collective-permute-start.27 = (bf16[256,128]{1,0:T(8,128)(2,1)S(1)}, bf16[256,128]{1,0:T(8,128)(2,1)S(1)}, u32[]{:S(2)}, u32[]{:S(2)}) collective-permute-start(bf16[256,128]{1,0:T(8,128)(2,1)S(1)} %get-tuple-element.83.refs_0_), channel_id=1, source_target_pairs={{0,4},{4,0},{8,12},{12,8},{1,5},{5,1},{9,13},{13,9},{2,6},{6,2},{1... | collective-permute-start | bytes 196616 | tf_op jit(solution)/shard_map/ppermute | solution.py:34
  52.9 2.8 %collective-permute-start.14 = (bf16[256,128]{1,0:T(8,128)(2,1)S(1)}, bf16[256,128]{1,0:T(8,128)(2,1)S(1)}, u32[]{:S(2)}, u32[]{:S(2)}) collective-permute-start(bf16[256,128]{1,0:T(8,128)(2,1)S(1)} %get-tuple-element.74.refs_0_), channel_id=1, source_target_pairs={{0,12},{4,8},{8,4},{12,0},{1,13},{5,9},{9,5},{13,1},{2,14},{6,10},... | collective-permute-start | bytes 196616 | tf_op jit(solution)/shard_map/ppermute | solution.py:34
  55.7 1.7 %collective-permute-start.12 = (bf16[256,128]{1,0:T(8,128)(2,1)S(1)}, bf16[256,128]{1,0:T(8,128)(2,1)S(1)}, u32[]{:S(2)}, u32[]{:S(2)}) collective-permute-start(bf16[256,128]{1,0:T(8,128)(2,1)S(1)} %get-tuple-element.74.refs_0_), channel_id=1, source_target_pairs={{0,4},{4,0},{8,12},{12,8},{1,5},{5,1},{9,13},{13,9},{2,6},{6,2},{1... | collective-permute-start | bytes 196616 | tf_op jit(solution)/shard_map/ppermute | solution.py:34
  57.5 1.6 %copy-done.1 = bf16[16,256,256]{2,1,0:T(8,128)(2,1)S(1)} copy-done((bf16[16,256,256]{2,1,0:T(8,128)(2,1)S(1)}, bf16[16,256,256]{2,1,0:T(8,128)(2,1)}, u32[]{:S(2)}) %copy-start.1) | copy-done | bytes 2097176
  59.1 1.2 shard_map.125.refs_1_
  60.9 1.2 shard_map.120.refs_0_
  62.2 1.5 %collective-permute-done.30.refs_2_ = bf16[4,256,128]{2,1,0:T(8,128)(2,1)S(1)} collective-permute-done((bf16[4,256,128]{2,1,0:T(8,128)(2,1)S(1)}, bf16[4,256,128]{2,1,0:T(8,128)(2,1)S(1)}, u32[]{:S(2)}, u32[]{:S(2)}) %collective-permute-start.30) | collective-permute-done | bytes 262176 | tf_op jit(solution)/shard_map/ppermute | solution.py:34
  64.0 1.6 %collective-permute-start.31 = (bf16[256,128]{1,0:T(8,128)(2,1)S(1)}, bf16[256,128]{1,0:T(8,128)(2,1)S(1)}, u32[]{:S(2)}, u32[]{:S(2)}) collective-permute-start(bf16[256,128]{1,0:T(8,128)(2,1)S(1)} %get-tuple-element.85), channel_id=1, source_target_pairs={{0,1},{1,0},{2,3},{3,2},{4,5},{5,4},{6,7},{7,6},{8,9},{9,8},{10,11... | collective-permute-start | bytes 196616 | tf_op jit(solution)/shard_map/ppermute | solution.py:34
  65.6 1.5 %collective-permute-start.32 = (bf16[256,128]{1,0:T(8,128)(2,1)S(1)}, bf16[256,128]{1,0:T(8,128)(2,1)S(1)}, u32[]{:S(2)}, u32[]{:S(2)}) collective-permute-start(bf16[256,128]{1,0:T(8,128)(2,1)S(1)} %get-tuple-element.86), channel_id=1, source_target_pairs={{0,2},{1,3},{2,0},{3,1},{4,6},{5,7},{6,4},{7,5},{8,10},{9,11},{10,... | collective-permute-start | bytes 196616 | tf_op jit(solution)/shard_map/ppermute | solution.py:34
  68.3 1.5 %collective-permute-done.32.refs_2_ = bf16[256,128]{1,0:T(8,128)(2,1)S(1)} collective-permute-done((bf16[256,128]{1,0:T(8,128)(2,1)S(1)}, bf16[256,128]{1,0:T(8,128)(2,1)S(1)}, u32[]{:S(2)}, u32[]{:S(2)}) %collective-permute-start.32) | collective-permute-done | bytes 65568 | tf_op jit(solution)/shard_map/ppermute | solution.py:34
  69.8 2.4 %collective-permute-done.33.refs_3_ = bf16[256,128]{1,0:T(8,128)(2,1)S(1)} collective-permute-done((bf16[256,128]{1,0:T(8,128)(2,1)S(1)}, bf16[256,128]{1,0:T(8,128)(2,1)S(1)}, u32[]{:S(2)}, u32[]{:S(2)}) %collective-permute-start.33) | collective-permute-done | bytes 65568 | tf_op jit(solution)/shard_map/ppermute | solution.py:34
  73.7 1.5 %collective-permute-start.36 = (bf16[128,256]{1,0:T(8,128)(2,1)S(1)}, bf16[128,256]{1,0:T(8,128)(2,1)S(1)}, u32[]{:S(2)}, u32[]{:S(2)}) collective-permute-start(bf16[128,256]{1,0:T(8,128)(2,1)S(1)} %get-tuple-element.91.refs_0_), channel_id=1, source_target_pairs={{0,2},{1,3},{2,0},{3,1},{4,6},{5,7},{6,4},{7,5},{8,10},{9,11},{10,... | collective-permute-start | bytes 196616 | tf_op jit(solution)/shard_map/ppermute | solution.py:34
  75.2 1.5 %collective-permute-start.35 = (bf16[128,256]{1,0:T(8,128)(2,1)S(1)}, bf16[128,256]{1,0:T(8,128)(2,1)S(1)}, u32[]{:S(2)}, u32[]{:S(2)}) collective-permute-start(bf16[128,256]{1,0:T(8,128)(2,1)S(1)} %get-tuple-element.91.refs_0_), channel_id=1, source_target_pairs={{0,1},{1,0},{2,3},{3,2},{4,5},{5,4},{6,7},{7,6},{8,9},{9,8},{10,11... | collective-permute-start | bytes 196616 | tf_op jit(solution)/shard_map/ppermute | solution.py:34
  76.7 1.8 %collective-permute-done.37.refs_3_ = bf16[128,256]{1,0:T(8,128)(2,1)S(1)} collective-permute-done((bf16[128,256]{1,0:T(8,128)(2,1)S(1)}, bf16[128,256]{1,0:T(8,128)(2,1)S(1)}, u32[]{:S(2)}, u32[]{:S(2)}) %collective-permute-start.37) | collective-permute-done | bytes 65568 | tf_op jit(solution)/shard_map/ppermute | solution.py:34
  79.4 1.0 shard_map.129
  81.3 2.1 %collective-permute-start.39 = (bf16[128,256]{1,0:T(8,128)(2,1)S(1)}, bf16[128,256]{1,0:T(8,128)(2,1)S(1)}, u32[]{:S(2)}, u32[]{:S(2)}) collective-permute-start(bf16[128,256]{1,0:T(8,128)(2,1)S(1)} %get-tuple-element.94), channel_id=1, source_target_pairs={{0,8},{4,12},{8,0},{12,4},{1,9},{5,13},{9,1},{13,5},{2,10},{6,14},... | collective-permute-start | bytes 196616 | tf_op jit(solution)/shard_map/ppermute | solution.py:34
  83.4 1.5 %collective-permute-start.40 = (bf16[128,256]{1,0:T(8,128)(2,1)S(1)}, bf16[128,256]{1,0:T(8,128)(2,1)S(1)}, u32[]{:S(2)}, u32[]{:S(2)}) collective-permute-start(bf16[128,256]{1,0:T(8,128)(2,1)S(1)} %get-tuple-element.95), channel_id=1, source_target_pairs={{0,12},{4,8},{8,4},{12,0},{1,13},{5,9},{9,5},{13,1},{2,14},{6,10},... | collective-permute-start | bytes 196616 | tf_op jit(solution)/shard_map/ppermute | solution.py:34
  84.9 1.0 shard_map.131
  86.0 2.9 %collective-permute-start.46 = (bf16[128,256]{1,0:T(8,128)(2,1)S(1)}, bf16[128,256]{1,0:T(8,128)(2,1)S(1)}, u32[]{:S(2)}, u32[]{:S(2)}) collective-permute-start(bf16[128,256]{1,0:T(8,128)(2,1)S(1)} %get-tuple-element.99), channel_id=1, source_target_pairs={{0,8},{4,12},{8,0},{12,4},{1,9},{5,13},{9,1},{13,5},{2,10},{6,14},... | collective-permute-start | bytes 196616 | tf_op jit(solution)/shard_map/ppermute | solution.py:34
  88.9 1.5 %collective-permute-start.47 = (bf16[128,256]{1,0:T(8,128)(2,1)S(1)}, bf16[128,256]{1,0:T(8,128)(2,1)S(1)}, u32[]{:S(2)}, u32[]{:S(2)}) collective-permute-start(bf16[128,256]{1,0:T(8,128)(2,1)S(1)} %get-tuple-element.100), channel_id=1, source_target_pairs={{0,12},{4,8},{8,4},{12,0},{1,13},{5,9},{9,5},{13,1},{2,14},{6,10},... | collective-permute-start | bytes 196616 | tf_op jit(solution)/shard_map/ppermute | solution.py:34
  90.7 1.5 %collective-permute-start.50 = (bf16[128,256]{1,0:T(8,128)(2,1)S(1)}, bf16[128,256]{1,0:T(8,128)(2,1)S(1)}, u32[]{:S(2)}, u32[]{:S(2)}) collective-permute-start(bf16[128,256]{1,0:T(8,128)(2,1)S(1)} %get-tuple-element.102.refs_0_), channel_id=1, source_target_pairs={{0,3},{1,2},{2,1},{3,0},{4,7},{5,6},{6,5},{7,4},{8,11},{9,10},{10,... | collective-permute-start | bytes 196616 | tf_op jit(solution)/shard_map/ppermute | solution.py:34
  92.2 1.5 %collective-permute-start.49 = (bf16[128,256]{1,0:T(8,128)(2,1)S(1)}, bf16[128,256]{1,0:T(8,128)(2,1)S(1)}, u32[]{:S(2)}, u32[]{:S(2)}) collective-permute-start(bf16[128,256]{1,0:T(8,128)(2,1)S(1)} %get-tuple-element.102.refs_0_), channel_id=1, source_target_pairs={{0,2},{1,3},{2,0},{3,1},{4,6},{5,7},{6,4},{7,5},{8,10},{9,11},{10,... | collective-permute-start | bytes 196616 | tf_op jit(solution)/shard_map/ppermute | solution.py:34
  95.4 1.5 %collective-permute-start.62 = (bf16[128,256]{1,0:T(8,128)(2,1)S(1)}, bf16[128,256]{1,0:T(8,128)(2,1)S(1)}, u32[]{:S(2)}, u32[]{:S(2)}) collective-permute-start(bf16[128,256]{1,0:T(8,128)(2,1)S(1)} %get-tuple-element.111.refs_0_), channel_id=1, source_target_pairs={{0,3},{1,2},{2,1},{3,0},{4,7},{5,6},{6,5},{7,4},{8,11},{9,10},{10,... | collective-permute-start | bytes 196616 | tf_op jit(solution)/shard_map/ppermute | solution.py:34
  96.9 1.5 %collective-permute-start.61 = (bf16[128,256]{1,0:T(8,128)(2,1)S(1)}, bf16[128,256]{1,0:T(8,128)(2,1)S(1)}, u32[]{:S(2)}, u32[]{:S(2)}) collective-permute-start(bf16[128,256]{1,0:T(8,128)(2,1)S(1)} %get-tuple-element.111.refs_0_), channel_id=1, source_target_pairs={{0,2},{1,3},{2,0},{3,1},{4,6},{5,7},{6,4},{7,5},{8,10},{9,11},{10,... | collective-permute-start | bytes 196616 | tf_op jit(solution)/shard_map/ppermute | solution.py:34
  98.9 1.0 shard_map.133
  100.0 2.2 %collective-permute-start.51 = (bf16[128,256]{1,0:T(8,128)(2,1)S(1)}, bf16[128,256]{1,0:T(8,128)(2,1)S(1)}, u32[]{:S(2)}, u32[]{:S(2)}) collective-permute-start(bf16[128,256]{1,0:T(8,128)(2,1)S(1)} %get-tuple-element.104), channel_id=1, source_target_pairs={{0,4},{4,0},{8,12},{12,8},{1,5},{5,1},{9,13},{13,9},{2,6},{6,2},{1... | collective-permute-start | bytes 196616 | tf_op jit(solution)/shard_map/ppermute | solution.py:34
  102.2 1.7 %collective-permute-start.52 = (bf16[128,256]{1,0:T(8,128)(2,1)S(1)}, bf16[128,256]{1,0:T(8,128)(2,1)S(1)}, u32[]{:S(2)}, u32[]{:S(2)}) collective-permute-start(bf16[128,256]{1,0:T(8,128)(2,1)S(1)} %get-tuple-element.105), channel_id=1, source_target_pairs={{0,8},{4,12},{8,0},{12,4},{1,9},{5,13},{9,1},{13,5},{2,10},{6,14},... | collective-permute-start | bytes 196616 | tf_op jit(solution)/shard_map/ppermute | solution.py:34
  103.9 1.4 %collective-permute-start.53 = (bf16[128,256]{1,0:T(8,128)(2,1)S(1)}, bf16[128,256]{1,0:T(8,128)(2,1)S(1)}, u32[]{:S(2)}, u32[]{:S(2)}) collective-permute-start(bf16[128,256]{1,0:T(8,128)(2,1)S(1)} %get-tuple-element.106), channel_id=1, source_target_pairs={{0,12},{4,8},{8,4},{12,0},{1,13},{5,9},{9,5},{13,1},{2,14},{6,10},... | collective-permute-start | bytes 196616 | tf_op jit(solution)/shard_map/ppermute | solution.py:34
  105.3 1.0 shard_map.137
  106.9 2.4 %collective-permute-start.64 = (bf16[128,256]{1,0:T(8,128)(2,1)S(1)}, bf16[128,256]{1,0:T(8,128)(2,1)S(1)}, u32[]{:S(2)}, u32[]{:S(2)}) collective-permute-start(bf16[128,256]{1,0:T(8,128)(2,1)S(1)} %get-tuple-element.114), channel_id=1, source_target_pairs={{0,8},{4,12},{8,0},{12,4},{1,9},{5,13},{9,1},{13,5},{2,10},{6,14},... | collective-permute-start | bytes 196616 | tf_op jit(solution)/shard_map/ppermute | solution.py:34
  109.4 1.4 %collective-permute-start.65 = (bf16[128,256]{1,0:T(8,128)(2,1)S(1)}, bf16[128,256]{1,0:T(8,128)(2,1)S(1)}, u32[]{:S(2)}, u32[]{:S(2)}) collective-permute-start(bf16[128,256]{1,0:T(8,128)(2,1)S(1)} %get-tuple-element.115), channel_id=1, source_target_pairs={{0,12},{4,8},{8,4},{12,0},{1,13},{5,9},{9,5},{13,1},{2,14},{6,10},... | collective-permute-start | bytes 196616 | tf_op jit(solution)/shard_map/ppermute | solution.py:34
  111.1 2.2 %collective-permute-start.56 = (bf16[128,256]{1,0:T(8,128)(2,1)S(1)}, bf16[128,256]{1,0:T(8,128)(2,1)S(1)}, u32[]{:S(2)}, u32[]{:S(2)}) collective-permute-start(bf16[128,256]{1,0:T(8,128)(2,1)S(1)} %shard_map.134.refs_0_), channel_id=1, source_target_pairs={{0,3},{1,2},{2,1},{3,0},{4,7},{5,6},{6,5},{7,4},{8,11},{9,10},{10,... | collective-permute-start | bytes 196616 | tf_op jit(solution)/shard_map/ppermute | solution.py:34
  115.7 2.2 %collective-permute-start.68 = (bf16[128,256]{1,0:T(8,128)(2,1)S(1)}, bf16[128,256]{1,0:T(8,128)(2,1)S(1)}, u32[]{:S(2)}, u32[]{:S(2)}) collective-permute-start(bf16[128,256]{1,0:T(8,128)(2,1)S(1)} %shard_map.138.refs_0_), channel_id=1, source_target_pairs={{0,3},{1,2},{2,1},{3,0},{4,7},{5,6},{6,5},{7,4},{8,11},{9,10},{10,... | collective-permute-start | bytes 196616 | tf_op jit(solution)/shard_map/ppermute | solution.py:34
  119.3 1.0 shard_map.135
  120.3 1.5 %collective-permute-start.58 = (bf16[128,256]{1,0:T(8,128)(2,1)S(1)}, bf16[128,256]{1,0:T(8,128)(2,1)S(1)}, u32[]{:S(2)}, u32[]{:S(2)}) collective-permute-start(bf16[128,256]{1,0:T(8,128)(2,1)S(1)} %get-tuple-element.110), channel_id=1, source_target_pairs={{0,4},{4,0},{8,12},{12,8},{1,5},{5,1},{9,13},{13,9},{2,6},{6,2},{1... | collective-permute-start | bytes 196616 | tf_op jit(solution)/shard_map/ppermute | solution.py:34
  123.0 1.0 shard_map.139
  124.0 1.4 %collective-permute-start.70 = (bf16[128,256]{1,0:T(8,128)(2,1)S(1)}, bf16[128,256]{1,0:T(8,128)(2,1)S(1)}, u32[]{:S(2)}, u32[]{:S(2)}) collective-permute-start(bf16[128,256]{1,0:T(8,128)(2,1)S(1)} %get-tuple-element.119), channel_id=1, source_target_pairs={{0,4},{4,0},{8,12},{12,8},{1,5},{5,1},{9,13},{13,9},{2,6},{6,2},{1... | collective-permute-start | bytes 196616 | tf_op jit(solution)/shard_map/ppermute | solution.py:34
  126.1 2.4 %collective-permute-start.59 = (bf16[128,256]{1,0:T(8,128)(2,1)S(1)}, bf16[128,256]{1,0:T(8,128)(2,1)S(1)}, u32[]{:S(2)}, u32[]{:S(2)}) collective-permute-start(bf16[128,256]{1,0:T(8,128)(2,1)S(1)} %shard_map.136), channel_id=1, source_target_pairs={{0,8},{4,12},{8,0},{12,4},{1,9},{5,13},{9,1},{13,5},{2,10},{6,14},... | collective-permute-start | bytes 196616 | tf_op jit(solution)/shard_map/ppermute | solution.py:34
  128.7 2.7 %collective-permute-start.71 = (bf16[128,256]{1,0:T(8,128)(2,1)S(1)}, bf16[128,256]{1,0:T(8,128)(2,1)S(1)}, u32[]{:S(2)}, u32[]{:S(2)}) collective-permute-start(bf16[128,256]{1,0:T(8,128)(2,1)S(1)} %shard_map.140), channel_id=1, source_target_pairs={{0,8},{4,12},{8,0},{12,4},{1,9},{5,13},{9,1},{13,5},{2,10},{6,14},... | collective-permute-start | bytes 196616 | tf_op jit(solution)/shard_map/ppermute | solution.py:34
  131.5 1.3 collective-permute-done.69.refs_8_
  132.8 1.4 %collective-permute-done.71.refs_9_ = bf16[128,256]{1,0:T(8,128)(2,1)S(1)} collective-permute-done((bf16[128,256]{1,0:T(8,128)(2,1)S(1)}, bf16[128,256]{1,0:T(8,128)(2,1)S(1)}, u32[]{:S(2)}, u32[]{:S(2)}) %collective-permute-start.71) | collective-permute-done | bytes 65568 | tf_op jit(solution)/shard_map/ppermute | solution.py:34
  134.2 1.3 shard_map.141
  (135 shorter events, 24.1 us)
Async XLA Ops:
  3.4 9.5 %collective-permute-start.17 = (bf16[256,128]{1,0:T(8,128)(2,1)S(1)}, bf16[256,128]{1,0:T(8,128)(2,1)S(1)}, u32[]{:S(2)}, u32[]{:S(2)}) collective-permute-start(bf16[256,128]{1,0:T(8,128)(2,1)S(1)} %shard_map.114.after_ref.refs_0_), channel_id=1, source_target_pairs={{0,12},{4,8},{8,4},{12,0},{1,13},{5,9},{9,5},{13,1},{2,14},{6,10},... | collective-permute-start | bytes 196616 | tf_op jit(solution)/shard_map/ppermute | solution.py:34
  8.5 8.5 %collective-permute-start.16 = (bf16[256,128]{1,0:T(8,128)(2,1)S(1)}, bf16[256,128]{1,0:T(8,128)(2,1)S(1)}, u32[]{:S(2)}, u32[]{:S(2)}) collective-permute-start(bf16[256,128]{1,0:T(8,128)(2,1)S(1)} %shard_map.114.after_ref.refs_0_), channel_id=1, source_target_pairs={{0,8},{4,12},{8,0},{12,4},{1,9},{5,13},{9,1},{13,5},{2,10},{6,14},... | collective-permute-start | bytes 196616 | tf_op jit(solution)/shard_map/ppermute | solution.py:34
  8.5 8.5 %collective-permute-start.15 = (bf16[256,128]{1,0:T(8,128)(2,1)S(1)}, bf16[256,128]{1,0:T(8,128)(2,1)S(1)}, u32[]{:S(2)}, u32[]{:S(2)}) collective-permute-start(bf16[256,128]{1,0:T(8,128)(2,1)S(1)} %shard_map.114.after_ref.refs_0_), channel_id=1, source_target_pairs={{0,4},{4,0},{8,12},{12,8},{1,5},{5,1},{9,13},{13,9},{2,6},{6,2},{1... | collective-permute-start | bytes 196616 | tf_op jit(solution)/shard_map/ppermute | solution.py:34
  9.2 12.0 %collective-permute-start.2 = (bf16[256,128]{1,0:T(8,128)(2,1)S(1)}, bf16[256,128]{1,0:T(8,128)(2,1)S(1)}, u32[]{:S(2)}, u32[]{:S(2)}) collective-permute-start(bf16[256,128]{1,0:T(8,128)(2,1)S(1)} %get-tuple-element.64.refs_0_), channel_id=1, source_target_pairs={{0,12},{4,8},{8,4},{12,0},{1,13},{5,9},{9,5},{13,1},{2,14},{6,10},... | collective-permute-start | bytes 196616 | tf_op jit(solution)/shard_map/ppermute | solution.py:34
  12.9 8.9 %collective-permute-start.1 = (bf16[256,128]{1,0:T(8,128)(2,1)S(1)}, bf16[256,128]{1,0:T(8,128)(2,1)S(1)}, u32[]{:S(2)}, u32[]{:S(2)}) collective-permute-start(bf16[256,128]{1,0:T(8,128)(2,1)S(1)} %get-tuple-element.64.refs_0_), channel_id=1, source_target_pairs={{0,8},{4,12},{8,0},{12,4},{1,9},{5,13},{9,1},{13,5},{2,10},{6,14},... | collective-permute-start | bytes 196616 | tf_op jit(solution)/shard_map/ppermute | solution.py:34
  12.9 8.9 %collective-permute-start = (bf16[256,128]{1,0:T(8,128)(2,1)S(1)}, bf16[256,128]{1,0:T(8,128)(2,1)S(1)}, u32[]{:S(2)}, u32[]{:S(2)}) collective-permute-start(bf16[256,128]{1,0:T(8,128)(2,1)S(1)} %get-tuple-element.64.refs_0_), channel_id=1, source_target_pairs={{0,4},{4,0},{8,12},{12,8},{1,5},{5,1},{9,13},{13,9},{2,6},{6,2},{1... | collective-permute-start | bytes 196616 | tf_op jit(solution)/shard_map/ppermute | solution.py:34
  18.3 7.7 %collective-permute-start.18 = (bf16[256,128]{1,0:T(8,128)(2,1)S(1)}, bf16[256,128]{1,0:T(8,128)(2,1)S(1)}, u32[]{:S(2)}, u32[]{:S(2)}) collective-permute-start(bf16[256,128]{1,0:T(8,128)(2,1)S(1)} %get-tuple-element.76), channel_id=1, source_target_pairs={{0,1},{1,0},{2,3},{3,2},{4,5},{5,4},{6,7},{7,6},{8,9},{9,8},{10,11... | collective-permute-start | bytes 196616 | tf_op jit(solution)/shard_map/ppermute | solution.py:34
  19.6 7.1 %collective-permute-start.19 = (bf16[256,128]{1,0:T(8,128)(2,1)S(1)}, bf16[256,128]{1,0:T(8,128)(2,1)S(1)}, u32[]{:S(2)}, u32[]{:S(2)}) collective-permute-start(bf16[256,128]{1,0:T(8,128)(2,1)S(1)} %get-tuple-element.77), channel_id=1, source_target_pairs={{0,2},{1,3},{2,0},{3,1},{4,6},{5,7},{6,4},{7,5},{8,10},{9,11},{10,... | collective-permute-start | bytes 196616 | tf_op jit(solution)/shard_map/ppermute | solution.py:34
  21.1 5.5 %collective-permute-start.20 = (bf16[256,128]{1,0:T(8,128)(2,1)S(1)}, bf16[256,128]{1,0:T(8,128)(2,1)S(1)}, u32[]{:S(2)}, u32[]{:S(2)}) collective-permute-start(bf16[256,128]{1,0:T(8,128)(2,1)S(1)} %get-tuple-element.78), channel_id=1, source_target_pairs={{0,3},{1,2},{2,1},{3,0},{4,7},{5,6},{6,5},{7,4},{8,11},{9,10},{10,... | collective-permute-start | bytes 196616 | tf_op jit(solution)/shard_map/ppermute | solution.py:34
  23.1 6.9 %collective-permute-start.3 = (bf16[256,128]{1,0:T(8,128)(2,1)S(1)}, bf16[256,128]{1,0:T(8,128)(2,1)S(1)}, u32[]{:S(2)}, u32[]{:S(2)}) collective-permute-start(bf16[256,128]{1,0:T(8,128)(2,1)S(1)} %get-tuple-element.66), channel_id=1, source_target_pairs={{0,1},{1,0},{2,3},{3,2},{4,5},{5,4},{6,7},{7,6},{8,9},{9,8},{10,11... | collective-permute-start | bytes 196616 | tf_op jit(solution)/shard_map/ppermute | solution.py:34
  24.4 7.1 %collective-permute-start.4 = (bf16[256,128]{1,0:T(8,128)(2,1)S(1)}, bf16[256,128]{1,0:T(8,128)(2,1)S(1)}, u32[]{:S(2)}, u32[]{:S(2)}) collective-permute-start(bf16[256,128]{1,0:T(8,128)(2,1)S(1)} %get-tuple-element.67), channel_id=1, source_target_pairs={{0,2},{1,3},{2,0},{3,1},{4,6},{5,7},{6,4},{7,5},{8,10},{9,11},{10,... | collective-permute-start | bytes 196616 | tf_op jit(solution)/shard_map/ppermute | solution.py:34
  26.0 5.6 %collective-permute-start.5 = (bf16[256,128]{1,0:T(8,128)(2,1)S(1)}, bf16[256,128]{1,0:T(8,128)(2,1)S(1)}, u32[]{:S(2)}, u32[]{:S(2)}) collective-permute-start(bf16[256,128]{1,0:T(8,128)(2,1)S(1)} %get-tuple-element.68), channel_id=1, source_target_pairs={{0,3},{1,2},{2,1},{3,0},{4,7},{5,6},{6,5},{7,4},{8,11},{9,10},{10,... | collective-permute-start | bytes 196616 | tf_op jit(solution)/shard_map/ppermute | solution.py:34
  27.1 7.8 %collective-permute-start.23 = (bf16[256,128]{1,0:T(8,128)(2,1)S(1)}, bf16[256,128]{1,0:T(8,128)(2,1)S(1)}, u32[]{:S(2)}, u32[]{:S(2)}) collective-permute-start(bf16[256,128]{1,0:T(8,128)(2,1)S(1)} %shard_map.122.refs_0_), channel_id=1, source_target_pairs={{0,12},{4,8},{8,4},{12,0},{1,13},{5,9},{9,5},{13,1},{2,14},{6,10},... | collective-permute-start | bytes 196616 | tf_op jit(solution)/shard_map/ppermute | solution.py:34
  30.0 6.5 %collective-permute-start.22 = (bf16[256,128]{1,0:T(8,128)(2,1)S(1)}, bf16[256,128]{1,0:T(8,128)(2,1)S(1)}, u32[]{:S(2)}, u32[]{:S(2)}) collective-permute-start(bf16[256,128]{1,0:T(8,128)(2,1)S(1)} %shard_map.122.refs_0_), channel_id=1, source_target_pairs={{0,8},{4,12},{8,0},{12,4},{1,9},{5,13},{9,1},{13,5},{2,10},{6,14},... | collective-permute-start | bytes 196616 | tf_op jit(solution)/shard_map/ppermute | solution.py:34
  30.0 6.5 %collective-permute-start.21 = (bf16[256,128]{1,0:T(8,128)(2,1)S(1)}, bf16[256,128]{1,0:T(8,128)(2,1)S(1)}, u32[]{:S(2)}, u32[]{:S(2)}) collective-permute-start(bf16[256,128]{1,0:T(8,128)(2,1)S(1)} %shard_map.122.refs_0_), channel_id=1, source_target_pairs={{0,4},{4,0},{8,12},{12,8},{1,5},{5,1},{9,13},{13,9},{2,6},{6,2},{1... | collective-permute-start | bytes 196616 | tf_op jit(solution)/shard_map/ppermute | solution.py:34
  31.9 8.9 %collective-permute-start.8 = (bf16[256,128]{1,0:T(8,128)(2,1)S(1)}, bf16[256,128]{1,0:T(8,128)(2,1)S(1)}, u32[]{:S(2)}, u32[]{:S(2)}) collective-permute-start(bf16[256,128]{1,0:T(8,128)(2,1)S(1)} %shard_map.117.refs_0_), channel_id=1, source_target_pairs={{0,12},{4,8},{8,4},{12,0},{1,13},{5,9},{9,5},{13,1},{2,14},{6,10},... | collective-permute-start | bytes 196616 | tf_op jit(solution)/shard_map/ppermute | solution.py:34
  34.8 6.5 %collective-permute-start.7 = (bf16[256,128]{1,0:T(8,128)(2,1)S(1)}, bf16[256,128]{1,0:T(8,128)(2,1)S(1)}, u32[]{:S(2)}, u32[]{:S(2)}) collective-permute-start(bf16[256,128]{1,0:T(8,128)(2,1)S(1)} %shard_map.117.refs_0_), channel_id=1, source_target_pairs={{0,8},{4,12},{8,0},{12,4},{1,9},{5,13},{9,1},{13,5},{2,10},{6,14},... | collective-permute-start | bytes 196616 | tf_op jit(solution)/shard_map/ppermute | solution.py:34
  34.8 6.5 %collective-permute-start.6 = (bf16[256,128]{1,0:T(8,128)(2,1)S(1)}, bf16[256,128]{1,0:T(8,128)(2,1)S(1)}, u32[]{:S(2)}, u32[]{:S(2)}) collective-permute-start(bf16[256,128]{1,0:T(8,128)(2,1)S(1)} %shard_map.117.refs_0_), channel_id=1, source_target_pairs={{0,4},{4,0},{8,12},{12,8},{1,5},{5,1},{9,13},{13,9},{2,6},{6,2},{1... | collective-permute-start | bytes 196616 | tf_op jit(solution)/shard_map/ppermute | solution.py:34
  37.7 9.3 %collective-permute-start.24 = (bf16[256,128]{1,0:T(8,128)(2,1)S(1)}, bf16[256,128]{1,0:T(8,128)(2,1)S(1)}, u32[]{:S(2)}, u32[]{:S(2)}) collective-permute-start(bf16[256,128]{1,0:T(8,128)(2,1)S(1)} %get-tuple-element.80), channel_id=1, source_target_pairs={{0,1},{1,0},{2,3},{3,2},{4,5},{5,4},{6,7},{7,6},{8,9},{9,8},{10,11... | collective-permute-start | bytes 196616 | tf_op jit(solution)/shard_map/ppermute | solution.py:34
  39.3 8.3 %collective-permute-start.25 = (bf16[256,128]{1,0:T(8,128)(2,1)S(1)}, bf16[256,128]{1,0:T(8,128)(2,1)S(1)}, u32[]{:S(2)}, u32[]{:S(2)}) collective-permute-start(bf16[256,128]{1,0:T(8,128)(2,1)S(1)} %get-tuple-element.81), channel_id=1, source_target_pairs={{0,2},{1,3},{2,0},{3,1},{4,6},{5,7},{6,4},{7,5},{8,10},{9,11},{10,... | collective-permute-start | bytes 196616 | tf_op jit(solution)/shard_map/ppermute | solution.py:34
  40.8 6.7 %collective-permute-start.26 = (bf16[256,128]{1,0:T(8,128)(2,1)S(1)}, bf16[256,128]{1,0:T(8,128)(2,1)S(1)}, u32[]{:S(2)}, u32[]{:S(2)}) collective-permute-start(bf16[256,128]{1,0:T(8,128)(2,1)S(1)} %get-tuple-element.82), channel_id=1, source_target_pairs={{0,3},{1,2},{2,1},{3,0},{4,7},{5,6},{6,5},{7,4},{8,11},{9,10},{10,... | collective-permute-start | bytes 196616 | tf_op jit(solution)/shard_map/ppermute | solution.py:34
  44.0 6.8 %collective-permute-start.9 = (bf16[256,128]{1,0:T(8,128)(2,1)S(1)}, bf16[256,128]{1,0:T(8,128)(2,1)S(1)}, u32[]{:S(2)}, u32[]{:S(2)}) collective-permute-start(bf16[256,128]{1,0:T(8,128)(2,1)S(1)} %get-tuple-element.71), channel_id=1, source_target_pairs={{0,1},{1,0},{2,3},{3,2},{4,5},{5,4},{6,7},{7,6},{8,9},{9,8},{10,11... | collective-permute-start | bytes 196616 | tf_op jit(solution)/shard_map/ppermute | solution.py:34
  45.5 6.9 %collective-permute-start.10 = (bf16[256,128]{1,0:T(8,128)(2,1)S(1)}, bf16[256,128]{1,0:T(8,128)(2,1)S(1)}, u32[]{:S(2)}, u32[]{:S(2)}) collective-permute-start(bf16[256,128]{1,0:T(8,128)(2,1)S(1)} %get-tuple-element.72), channel_id=1, source_target_pairs={{0,2},{1,3},{2,0},{3,1},{4,6},{5,7},{6,4},{7,5},{8,10},{9,11},{10,... | collective-permute-start | bytes 196616 | tf_op jit(solution)/shard_map/ppermute | solution.py:34
  47.0 5.4 %collective-permute-start.11 = (bf16[256,128]{1,0:T(8,128)(2,1)S(1)}, bf16[256,128]{1,0:T(8,128)(2,1)S(1)}, u32[]{:S(2)}, u32[]{:S(2)}) collective-permute-start(bf16[256,128]{1,0:T(8,128)(2,1)S(1)} %get-tuple-element.73), channel_id=1, source_target_pairs={{0,3},{1,2},{2,1},{3,0},{4,7},{5,6},{6,5},{7,4},{8,11},{9,10},{10,... | collective-permute-start | bytes 196616 | tf_op jit(solution)/shard_map/ppermute | solution.py:34
  48.0 7.7 %collective-permute-start.29 = (bf16[256,128]{1,0:T(8,128)(2,1)S(1)}, bf16[256,128]{1,0:T(8,128)(2,1)S(1)}, u32[]{:S(2)}, u32[]{:S(2)}) collective-permute-start(bf16[256,128]{1,0:T(8,128)(2,1)S(1)} %get-tuple-element.83.refs_0_), channel_id=1, source_target_pairs={{0,12},{4,8},{8,4},{12,0},{1,13},{5,9},{9,5},{13,1},{2,14},{6,10},... | collective-permute-start | bytes 196616 | tf_op jit(solution)/shard_map/ppermute | solution.py:34
  50.8 6.7 %collective-permute-start.28 = (bf16[256,128]{1,0:T(8,128)(2,1)S(1)}, bf16[256,128]{1,0:T(8,128)(2,1)S(1)}, u32[]{:S(2)}, u32[]{:S(2)}) collective-permute-start(bf16[256,128]{1,0:T(8,128)(2,1)S(1)} %get-tuple-element.83.refs_0_), channel_id=1, source_target_pairs={{0,8},{4,12},{8,0},{12,4},{1,9},{5,13},{9,1},{13,5},{2,10},{6,14},... | collective-permute-start | bytes 196616 | tf_op jit(solution)/shard_map/ppermute | solution.py:34
  50.8 6.7 %collective-permute-start.27 = (bf16[256,128]{1,0:T(8,128)(2,1)S(1)}, bf16[256,128]{1,0:T(8,128)(2,1)S(1)}, u32[]{:S(2)}, u32[]{:S(2)}) collective-permute-start(bf16[256,128]{1,0:T(8,128)(2,1)S(1)} %get-tuple-element.83.refs_0_), channel_id=1, source_target_pairs={{0,4},{4,0},{8,12},{12,8},{1,5},{5,1},{9,13},{13,9},{2,6},{6,2},{1... | collective-permute-start | bytes 196616 | tf_op jit(solution)/shard_map/ppermute | solution.py:34
  52.9 7.5 %collective-permute-start.14 = (bf16[256,128]{1,0:T(8,128)(2,1)S(1)}, bf16[256,128]{1,0:T(8,128)(2,1)S(1)}, u32[]{:S(2)}, u32[]{:S(2)}) collective-permute-start(bf16[256,128]{1,0:T(8,128)(2,1)S(1)} %get-tuple-element.74.refs_0_), channel_id=1, source_target_pairs={{0,12},{4,8},{8,4},{12,0},{1,13},{5,9},{9,5},{13,1},{2,14},{6,10},... | collective-permute-start | bytes 196616 | tf_op jit(solution)/shard_map/ppermute | solution.py:34
  55.7 5.2 %collective-permute-start.13 = (bf16[256,128]{1,0:T(8,128)(2,1)S(1)}, bf16[256,128]{1,0:T(8,128)(2,1)S(1)}, u32[]{:S(2)}, u32[]{:S(2)}) collective-permute-start(bf16[256,128]{1,0:T(8,128)(2,1)S(1)} %get-tuple-element.74.refs_0_), channel_id=1, source_target_pairs={{0,8},{4,12},{8,0},{12,4},{1,9},{5,13},{9,1},{13,5},{2,10},{6,14},... | collective-permute-start | bytes 196616 | tf_op jit(solution)/shard_map/ppermute | solution.py:34
  55.7 5.2 %collective-permute-start.12 = (bf16[256,128]{1,0:T(8,128)(2,1)S(1)}, bf16[256,128]{1,0:T(8,128)(2,1)S(1)}, u32[]{:S(2)}, u32[]{:S(2)}) collective-permute-start(bf16[256,128]{1,0:T(8,128)(2,1)S(1)} %get-tuple-element.74.refs_0_), channel_id=1, source_target_pairs={{0,4},{4,0},{8,12},{12,8},{1,5},{5,1},{9,13},{13,9},{2,6},{6,2},{1... | collective-permute-start | bytes 196616 | tf_op jit(solution)/shard_map/ppermute | solution.py:34
  67.1 5.2 %collective-permute-start.33 = (bf16[256,128]{1,0:T(8,128)(2,1)S(1)}, bf16[256,128]{1,0:T(8,128)(2,1)S(1)}, u32[]{:S(2)}, u32[]{:S(2)}) collective-permute-start(bf16[256,128]{1,0:T(8,128)(2,1)S(1)} %get-tuple-element.87), channel_id=1, source_target_pairs={{0,3},{1,2},{2,1},{3,0},{4,7},{5,6},{6,5},{7,4},{8,11},{9,10},{10,... | collective-permute-start | bytes 196616 | tf_op jit(solution)/shard_map/ppermute | solution.py:34
  73.1 5.3 %collective-permute-start.37 = (bf16[128,256]{1,0:T(8,128)(2,1)S(1)}, bf16[128,256]{1,0:T(8,128)(2,1)S(1)}, u32[]{:S(2)}, u32[]{:S(2)}) collective-permute-start(bf16[128,256]{1,0:T(8,128)(2,1)S(1)} %get-tuple-element.91.refs_0_), channel_id=1, source_target_pairs={{0,3},{1,2},{2,1},{3,0},{4,7},{5,6},{6,5},{7,4},{8,11},{9,10},{10,... | collective-permute-start | bytes 196616 | tf_op jit(solution)/shard_map/ppermute | solution.py:34
  73.7 5.0 %collective-permute-start.36 = (bf16[128,256]{1,0:T(8,128)(2,1)S(1)}, bf16[128,256]{1,0:T(8,128)(2,1)S(1)}, u32[]{:S(2)}, u32[]{:S(2)}) collective-permute-start(bf16[128,256]{1,0:T(8,128)(2,1)S(1)} %get-tuple-element.91.refs_0_), channel_id=1, source_target_pairs={{0,2},{1,3},{2,0},{3,1},{4,6},{5,7},{6,4},{7,5},{8,10},{9,11},{10,... | collective-permute-start | bytes 196616 | tf_op jit(solution)/shard_map/ppermute | solution.py:34
  78.4 5.0 %collective-permute-start.44 = (bf16[128,256]{1,0:T(8,128)(2,1)S(1)}, bf16[128,256]{1,0:T(8,128)(2,1)S(1)}, u32[]{:S(2)}, u32[]{:S(2)}) collective-permute-start(bf16[128,256]{1,0:T(8,128)(2,1)S(1)} %collective-permute-done.37.refs_3_), channel_id=1, source_target_pairs={{0,16},{16,0},{1,17},{17,1},{2,18},{18,2},{3,19},{19,3},{4,20},{20... | collective-permute-start | bytes 196616 | tf_op jit(solution)/shard_map/ppermute | solution.py:34
  78.6 6.3 %collective-permute-start.43 = (bf16[128,256]{1,0:T(8,128)(2,1)S(1)}, bf16[128,256]{1,0:T(8,128)(2,1)S(1)}, u32[]{:S(2)}, u32[]{:S(2)}) collective-permute-start(bf16[128,256]{1,0:T(8,128)(2,1)S(1)} %collective-permute-done.36.refs_2_), channel_id=1, source_target_pairs={{0,16},{16,0},{1,17},{17,1},{2,18},{18,2},{3,19},{19,3},{4,20},{20... | collective-permute-start | bytes 196616 | tf_op jit(solution)/shard_map/ppermute | solution.py:34
  79.4 5.5 %collective-permute-start.42 = (bf16[128,256]{1,0:T(8,128)(2,1)S(1)}, bf16[128,256]{1,0:T(8,128)(2,1)S(1)}, u32[]{:S(2)}, u32[]{:S(2)}) collective-permute-start(bf16[128,256]{1,0:T(8,128)(2,1)S(1)} %collective-permute-done.35.refs_1_), channel_id=1, source_target_pairs={{0,16},{16,0},{1,17},{17,1},{2,18},{18,2},{3,19},{19,3},{4,20},{20... | collective-permute-start | bytes 196616 | tf_op jit(solution)/shard_map/ppermute | solution.py:34
  80.5 8.4 %collective-permute-start.38 = (bf16[128,256]{1,0:T(8,128)(2,1)S(1)}, bf16[128,256]{1,0:T(8,128)(2,1)S(1)}, u32[]{:S(2)}, u32[]{:S(2)}) collective-permute-start(bf16[128,256]{1,0:T(8,128)(2,1)S(1)} %get-tuple-element.93), channel_id=1, source_target_pairs={{0,4},{4,0},{8,12},{12,8},{1,5},{5,1},{9,13},{13,9},{2,6},{6,2},{1... | collective-permute-start | bytes 196616 | tf_op jit(solution)/shard_map/ppermute | solution.py:34
  81.3 9.1 %collective-permute-start.39 = (bf16[128,256]{1,0:T(8,128)(2,1)S(1)}, bf16[128,256]{1,0:T(8,128)(2,1)S(1)}, u32[]{:S(2)}, u32[]{:S(2)}) collective-permute-start(bf16[128,256]{1,0:T(8,128)(2,1)S(1)} %get-tuple-element.94), channel_id=1, source_target_pairs={{0,8},{4,12},{8,0},{12,4},{1,9},{5,13},{9,1},{13,5},{2,10},{6,14},... | collective-permute-start | bytes 196616 | tf_op jit(solution)/shard_map/ppermute | solution.py:34
  83.4 7.0 %collective-permute-start.40 = (bf16[128,256]{1,0:T(8,128)(2,1)S(1)}, bf16[128,256]{1,0:T(8,128)(2,1)S(1)}, u32[]{:S(2)}, u32[]{:S(2)}) collective-permute-start(bf16[128,256]{1,0:T(8,128)(2,1)S(1)} %get-tuple-element.95), channel_id=1, source_target_pairs={{0,12},{4,8},{8,4},{12,0},{1,13},{5,9},{9,5},{13,1},{2,14},{6,10},... | collective-permute-start | bytes 196616 | tf_op jit(solution)/shard_map/ppermute | solution.py:34
  85.9 7.8 %collective-permute-start.45 = (bf16[128,256]{1,0:T(8,128)(2,1)S(1)}, bf16[128,256]{1,0:T(8,128)(2,1)S(1)}, u32[]{:S(2)}, u32[]{:S(2)}) collective-permute-start(bf16[128,256]{1,0:T(8,128)(2,1)S(1)} %get-tuple-element.98), channel_id=1, source_target_pairs={{0,4},{4,0},{8,12},{12,8},{1,5},{5,1},{9,13},{13,9},{2,6},{6,2},{1... | collective-permute-start | bytes 196616 | tf_op jit(solution)/shard_map/ppermute | solution.py:34
  86.0 8.3 %collective-permute-start.46 = (bf16[128,256]{1,0:T(8,128)(2,1)S(1)}, bf16[128,256]{1,0:T(8,128)(2,1)S(1)}, u32[]{:S(2)}, u32[]{:S(2)}) collective-permute-start(bf16[128,256]{1,0:T(8,128)(2,1)S(1)} %get-tuple-element.99), channel_id=1, source_target_pairs={{0,8},{4,12},{8,0},{12,4},{1,9},{5,13},{9,1},{13,5},{2,10},{6,14},... | collective-permute-start | bytes 196616 | tf_op jit(solution)/shard_map/ppermute | solution.py:34
  88.9 6.2 %collective-permute-start.47 = (bf16[128,256]{1,0:T(8,128)(2,1)S(1)}, bf16[128,256]{1,0:T(8,128)(2,1)S(1)}, u32[]{:S(2)}, u32[]{:S(2)}) collective-permute-start(bf16[128,256]{1,0:T(8,128)(2,1)S(1)} %get-tuple-element.100), channel_id=1, source_target_pairs={{0,12},{4,8},{8,4},{12,0},{1,13},{5,9},{9,5},{13,1},{2,14},{6,10},... | collective-permute-start | bytes 196616 | tf_op jit(solution)/shard_map/ppermute | solution.py:34
  90.7 7.7 %collective-permute-start.50 = (bf16[128,256]{1,0:T(8,128)(2,1)S(1)}, bf16[128,256]{1,0:T(8,128)(2,1)S(1)}, u32[]{:S(2)}, u32[]{:S(2)}) collective-permute-start(bf16[128,256]{1,0:T(8,128)(2,1)S(1)} %get-tuple-element.102.refs_0_), channel_id=1, source_target_pairs={{0,3},{1,2},{2,1},{3,0},{4,7},{5,6},{6,5},{7,4},{8,11},{9,10},{10,... | collective-permute-start | bytes 196616 | tf_op jit(solution)/shard_map/ppermute | solution.py:34
  92.2 6.7 %collective-permute-start.49 = (bf16[128,256]{1,0:T(8,128)(2,1)S(1)}, bf16[128,256]{1,0:T(8,128)(2,1)S(1)}, u32[]{:S(2)}, u32[]{:S(2)}) collective-permute-start(bf16[128,256]{1,0:T(8,128)(2,1)S(1)} %get-tuple-element.102.refs_0_), channel_id=1, source_target_pairs={{0,2},{1,3},{2,0},{3,1},{4,6},{5,7},{6,4},{7,5},{8,10},{9,11},{10,... | collective-permute-start | bytes 196616 | tf_op jit(solution)/shard_map/ppermute | solution.py:34
  93.7 5.2 %collective-permute-start.48 = (bf16[128,256]{1,0:T(8,128)(2,1)S(1)}, bf16[128,256]{1,0:T(8,128)(2,1)S(1)}, u32[]{:S(2)}, u32[]{:S(2)}) collective-permute-start(bf16[128,256]{1,0:T(8,128)(2,1)S(1)} %get-tuple-element.102.refs_0_), channel_id=1, source_target_pairs={{0,1},{1,0},{2,3},{3,2},{4,5},{5,4},{6,7},{7,6},{8,9},{9,8},{10,11... | collective-permute-start | bytes 196616 | tf_op jit(solution)/shard_map/ppermute | solution.py:34
  95.4 8.5 %collective-permute-start.62 = (bf16[128,256]{1,0:T(8,128)(2,1)S(1)}, bf16[128,256]{1,0:T(8,128)(2,1)S(1)}, u32[]{:S(2)}, u32[]{:S(2)}) collective-permute-start(bf16[128,256]{1,0:T(8,128)(2,1)S(1)} %get-tuple-element.111.refs_0_), channel_id=1, source_target_pairs={{0,3},{1,2},{2,1},{3,0},{4,7},{5,6},{6,5},{7,4},{8,11},{9,10},{10,... | collective-permute-start | bytes 196616 | tf_op jit(solution)/shard_map/ppermute | solution.py:34
  96.9 8.4 %collective-permute-start.61 = (bf16[128,256]{1,0:T(8,128)(2,1)S(1)}, bf16[128,256]{1,0:T(8,128)(2,1)S(1)}, u32[]{:S(2)}, u32[]{:S(2)}) collective-permute-start(bf16[128,256]{1,0:T(8,128)(2,1)S(1)} %get-tuple-element.111.refs_0_), channel_id=1, source_target_pairs={{0,2},{1,3},{2,0},{3,1},{4,6},{5,7},{6,4},{7,5},{8,10},{9,11},{10,... | collective-permute-start | bytes 196616 | tf_op jit(solution)/shard_map/ppermute | solution.py:34
  98.4 6.9 %collective-permute-start.60 = (bf16[128,256]{1,0:T(8,128)(2,1)S(1)}, bf16[128,256]{1,0:T(8,128)(2,1)S(1)}, u32[]{:S(2)}, u32[]{:S(2)}) collective-permute-start(bf16[128,256]{1,0:T(8,128)(2,1)S(1)} %get-tuple-element.111.refs_0_), channel_id=1, source_target_pairs={{0,1},{1,0},{2,3},{3,2},{4,5},{5,4},{6,7},{7,6},{8,9},{9,8},{10,11... | collective-permute-start | bytes 196616 | tf_op jit(solution)/shard_map/ppermute | solution.py:34
  100.0 9.4 %collective-permute-start.51 = (bf16[128,256]{1,0:T(8,128)(2,1)S(1)}, bf16[128,256]{1,0:T(8,128)(2,1)S(1)}, u32[]{:S(2)}, u32[]{:S(2)}) collective-permute-start(bf16[128,256]{1,0:T(8,128)(2,1)S(1)} %get-tuple-element.104), channel_id=1, source_target_pairs={{0,4},{4,0},{8,12},{12,8},{1,5},{5,1},{9,13},{13,9},{2,6},{6,2},{1... | collective-permute-start | bytes 196616 | tf_op jit(solution)/shard_map/ppermute | solution.py:34
  102.2 8.6 %collective-permute-start.52 = (bf16[128,256]{1,0:T(8,128)(2,1)S(1)}, bf16[128,256]{1,0:T(8,128)(2,1)S(1)}, u32[]{:S(2)}, u32[]{:S(2)}) collective-permute-start(bf16[128,256]{1,0:T(8,128)(2,1)S(1)} %get-tuple-element.105), channel_id=1, source_target_pairs={{0,8},{4,12},{8,0},{12,4},{1,9},{5,13},{9,1},{13,5},{2,10},{6,14},... | collective-permute-start | bytes 196616 | tf_op jit(solution)/shard_map/ppermute | solution.py:34
  103.9 6.9 %collective-permute-start.53 = (bf16[128,256]{1,0:T(8,128)(2,1)S(1)}, bf16[128,256]{1,0:T(8,128)(2,1)S(1)}, u32[]{:S(2)}, u32[]{:S(2)}) collective-permute-start(bf16[128,256]{1,0:T(8,128)(2,1)S(1)} %get-tuple-element.106), channel_id=1, source_target_pairs={{0,12},{4,8},{8,4},{12,0},{1,13},{5,9},{9,5},{13,1},{2,14},{6,10},... | collective-permute-start | bytes 196616 | tf_op jit(solution)/shard_map/ppermute | solution.py:34
  106.3 7.8 %collective-permute-start.63 = (bf16[128,256]{1,0:T(8,128)(2,1)S(1)}, bf16[128,256]{1,0:T(8,128)(2,1)S(1)}, u32[]{:S(2)}, u32[]{:S(2)}) collective-permute-start(bf16[128,256]{1,0:T(8,128)(2,1)S(1)} %get-tuple-element.113), channel_id=1, source_target_pairs={{0,4},{4,0},{8,12},{12,8},{1,5},{5,1},{9,13},{13,9},{2,6},{6,2},{1... | collective-permute-start | bytes 196616 | tf_op jit(solution)/shard_map/ppermute | solution.py:34
  106.9 7.7 %collective-permute-start.64 = (bf16[128,256]{1,0:T(8,128)(2,1)S(1)}, bf16[128,256]{1,0:T(8,128)(2,1)S(1)}, u32[]{:S(2)}, u32[]{:S(2)}) collective-permute-start(bf16[128,256]{1,0:T(8,128)(2,1)S(1)} %get-tuple-element.114), channel_id=1, source_target_pairs={{0,8},{4,12},{8,0},{12,4},{1,9},{5,13},{9,1},{13,5},{2,10},{6,14},... | collective-permute-start | bytes 196616 | tf_op jit(solution)/shard_map/ppermute | solution.py:34
  109.4 6.1 %collective-permute-start.65 = (bf16[128,256]{1,0:T(8,128)(2,1)S(1)}, bf16[128,256]{1,0:T(8,128)(2,1)S(1)}, u32[]{:S(2)}, u32[]{:S(2)}) collective-permute-start(bf16[128,256]{1,0:T(8,128)(2,1)S(1)} %get-tuple-element.115), channel_id=1, source_target_pairs={{0,12},{4,8},{8,4},{12,0},{1,13},{5,9},{9,5},{13,1},{2,14},{6,10},... | collective-permute-start | bytes 196616 | tf_op jit(solution)/shard_map/ppermute | solution.py:34
  111.1 7.7 %collective-permute-start.56 = (bf16[128,256]{1,0:T(8,128)(2,1)S(1)}, bf16[128,256]{1,0:T(8,128)(2,1)S(1)}, u32[]{:S(2)}, u32[]{:S(2)}) collective-permute-start(bf16[128,256]{1,0:T(8,128)(2,1)S(1)} %shard_map.134.refs_0_), channel_id=1, source_target_pairs={{0,3},{1,2},{2,1},{3,0},{4,7},{5,6},{6,5},{7,4},{8,11},{9,10},{10,... | collective-permute-start | bytes 196616 | tf_op jit(solution)/shard_map/ppermute | solution.py:34
  113.2 6.0 %collective-permute-start.55 = (bf16[128,256]{1,0:T(8,128)(2,1)S(1)}, bf16[128,256]{1,0:T(8,128)(2,1)S(1)}, u32[]{:S(2)}, u32[]{:S(2)}) collective-permute-start(bf16[128,256]{1,0:T(8,128)(2,1)S(1)} %shard_map.134.refs_0_), channel_id=1, source_target_pairs={{0,2},{1,3},{2,0},{3,1},{4,6},{5,7},{6,4},{7,5},{8,10},{9,11},{10,... | collective-permute-start | bytes 196616 | tf_op jit(solution)/shard_map/ppermute | solution.py:34
  114.1 5.2 %collective-permute-start.54 = (bf16[128,256]{1,0:T(8,128)(2,1)S(1)}, bf16[128,256]{1,0:T(8,128)(2,1)S(1)}, u32[]{:S(2)}, u32[]{:S(2)}) collective-permute-start(bf16[128,256]{1,0:T(8,128)(2,1)S(1)} %shard_map.134.refs_0_), channel_id=1, source_target_pairs={{0,1},{1,0},{2,3},{3,2},{4,5},{5,4},{6,7},{7,6},{8,9},{9,8},{10,11... | collective-permute-start | bytes 196616 | tf_op jit(solution)/shard_map/ppermute | solution.py:34
  115.7 6.1 %collective-permute-start.68 = (bf16[128,256]{1,0:T(8,128)(2,1)S(1)}, bf16[128,256]{1,0:T(8,128)(2,1)S(1)}, u32[]{:S(2)}, u32[]{:S(2)}) collective-permute-start(bf16[128,256]{1,0:T(8,128)(2,1)S(1)} %shard_map.138.refs_0_), channel_id=1, source_target_pairs={{0,3},{1,2},{2,1},{3,0},{4,7},{5,6},{6,5},{7,4},{8,11},{9,10},{10,... | collective-permute-start | bytes 196616 | tf_op jit(solution)/shard_map/ppermute | solution.py:34
  119.3 12.2 %collective-permute-start.34 = (f32[128,256]{1,0:T(8,128)S(1)}, f32[128,256]{1,0:T(8,128)S(1)}, u32[]{:S(2)}, u32[]{:S(2)}) collective-permute-start(f32[128,256]{1,0:T(8,128)S(1)} %get-tuple-element.88.refs_0_), channel_id=1, source_target_pairs={{0,16},{16,0},{1,17},{17,1},{2,18},{18,2},{3,19},{19,3},{4,20},{20... | collective-permute-start | bytes 393224 | tf_op jit(solution)/shard_map/ppermute | solution.py:34
  120.3 5.8 %collective-permute-start.58 = (bf16[128,256]{1,0:T(8,128)(2,1)S(1)}, bf16[128,256]{1,0:T(8,128)(2,1)S(1)}, u32[]{:S(2)}, u32[]{:S(2)}) collective-permute-start(bf16[128,256]{1,0:T(8,128)(2,1)S(1)} %get-tuple-element.110), channel_id=1, source_target_pairs={{0,4},{4,0},{8,12},{12,8},{1,5},{5,1},{9,13},{13,9},{2,6},{6,2},{1... | collective-permute-start | bytes 196616 | tf_op jit(solution)/shard_map/ppermute | solution.py:34
  124.0 4.7 %collective-permute-start.70 = (bf16[128,256]{1,0:T(8,128)(2,1)S(1)}, bf16[128,256]{1,0:T(8,128)(2,1)S(1)}, u32[]{:S(2)}, u32[]{:S(2)}) collective-permute-start(bf16[128,256]{1,0:T(8,128)(2,1)S(1)} %get-tuple-element.119), channel_id=1, source_target_pairs={{0,4},{4,0},{8,12},{12,8},{1,5},{5,1},{9,13},{13,9},{2,6},{6,2},{1... | collective-permute-start | bytes 196616 | tf_op jit(solution)/shard_map/ppermute | solution.py:34
  125.5 6.0 %collective-permute-start.57 = (bf16[128,256]{1,0:T(8,128)(2,1)S(1)}, bf16[128,256]{1,0:T(8,128)(2,1)S(1)}, u32[]{:S(2)}, u32[]{:S(2)}) collective-permute-start(bf16[128,256]{1,0:T(8,128)(2,1)S(1)} %get-tuple-element.108), channel_id=1, source_target_pairs={{0,4},{4,0},{8,12},{12,8},{1,5},{5,1},{9,13},{13,9},{2,6},{6,2},{1... | collective-permute-start | bytes 196616 | tf_op jit(solution)/shard_map/ppermute | solution.py:34
  126.1 5.3 %collective-permute-start.59 = (bf16[128,256]{1,0:T(8,128)(2,1)S(1)}, bf16[128,256]{1,0:T(8,128)(2,1)S(1)}, u32[]{:S(2)}, u32[]{:S(2)}) collective-permute-start(bf16[128,256]{1,0:T(8,128)(2,1)S(1)} %shard_map.136), channel_id=1, source_target_pairs={{0,8},{4,12},{8,0},{12,4},{1,9},{5,13},{9,1},{13,5},{2,10},{6,14},... | collective-permute-start | bytes 196616 | tf_op jit(solution)/shard_map/ppermute | solution.py:34
  128.7 5.5 %collective-permute-start.71 = (bf16[128,256]{1,0:T(8,128)(2,1)S(1)}, bf16[128,256]{1,0:T(8,128)(2,1)S(1)}, u32[]{:S(2)}, u32[]{:S(2)}) collective-permute-start(bf16[128,256]{1,0:T(8,128)(2,1)S(1)} %shard_map.140), channel_id=1, source_target_pairs={{0,8},{4,12},{8,0},{12,4},{1,9},{5,13},{9,1},{13,5},{2,10},{6,14},... | collective-permute-start | bytes 196616 | tf_op jit(solution)/shard_map/ppermute | solution.py:34
  (19 other events, 131.6 us)
